TPU v7x, 32 devices: a whole 2x2x4 slice. The times are simulated.
32 devices in a mesh: dom: 8 (over y, x, core), sub: 4 (over z).
Axes of the slice: x: 2, y: 2, z: 4, core: 2. Of those that a mesh axis runs over, the one named last changes fastest.
Arguments:
- dof_values: float32 [56, 9, 4096], P(None, None, ('dom', 'sub')), may hold values from -0.6 to 0.6
- stiffness: float32 [3, 56, 56], replicated, may hold values from -0.75 to 0.75
- face_project: float32 [4, 21, 56], replicated, may hold values from -0.75 to 0.75
- face_lift: float32 [4, 56, 21], replicated, may hold values from -1.25 to 1.25
- face_rotate: float32 [3, 21, 21], replicated, may hold values from -1.25 to 1.25
- star_matrices: float32 [3, 9, 9, 4096], P(None, None, None, ('dom', 'sub')), may hold values from -2 to 2
- flux_local: float32 [4, 9, 9, 4096], P(None, None, None, ('dom', 'sub')), may hold values from -1.2 to 1.2
- flux_neighbour: float32 [4, 9, 9, 4096], P(None, None, None, ('dom', 'sub')), may hold values from -1.2 to 1.2
- cluster_labels: int32 [4096], P(('dom', 'sub')), may hold values from 0 to 1, as said below
- neighbour_index: int32 [4, 4096], P(None, ('dom', 'sub')), may hold values from 0 to 287, as said below
- neighbour_face: int32 [4, 4096], P(None, ('dom', 'sub')), may hold values from 0 to 3
- neighbour_orient: int32 [4, 4096], P(None, ('dom', 'sub')), may hold values from 0 to 2
- send_element: int32 [32, 160], P(('dom', 'sub')), may hold values from 0 to 127
- send_face: int32 [32, 160], P(('dom', 'sub')), may hold values from 0 to 3
Outputs:
- new_dofs: float32 [56, 9, 4096], P(None, None, ('dom', 'sub'))
Inputs may be any that keep to these rules, and one draw needn't show every extreme that they name: `cluster_labels`: 0 marks an element of the fine cluster, 1 of the coarse cluster. `neighbour_index`: values below 128 name an own element of the same device; value 128 + s names receive slot s of that device. Every receive slot of a device is named by exactly one face of that device's elements.
All inputs are finite; a program needn't handle non-finite values.
Results may differ from a plain program's by a relative error of at most 0.0001.
Values sent between devices are 32-bit elements; how exact they have to be, the bound alone decides.
No kernel may reach another device: no remote copies, remote signals or barrier semaphores. Data moves between devices by JAX's collectives and lax.ppermute only.
A program may use at most 128 MiB of HBM per device.

v0:
```python
import jax
import jax.numpy as jnp
from jax import lax
from jax.experimental import pallas as pl
from jax.experimental.pallas import tpu as pltpu
from jax.sharding import PartitionSpec as P

TAYLOR_TERMS = 6
HALO_CURVE = 64
HALO_PEER = 8
F32 = jnp.float32
BF16 = jnp.bfloat16
LANES = 128
KB = 64


def up(n, m):
    return -(-n // m) * m


def halves(x):
    hi = x.astype(BF16)
    return hi, (x - hi.astype(F32)).astype(BF16)


def dot(a, b):
    return jnp.dot(a, b, preferred_element_type=F32)


class Dims:
    def __init__(self, basis, nvar, elements, fbasis, slots, subs):
        self.basis, self.nvar, self.elements, self.fbasis = basis, nvar, elements, fbasis
        self.slots, self.subs = slots, subs
        self.mp = up(fbasis, 8)
        self.fm = 4 * self.mp
        self.rows = nvar * self.mp
        self.width = nvar * elements
        self.cols4 = 4 * elements
        self.slot_cols = up(slots, LANES)
        self.half = up(-(-self.rows // 2), 8)
        self.rows_pad = up(self.rows, LANES)
        self.left_rows = self.fm + 3 * basis
        self.groups = []
        r0 = 0
        while r0 < basis:
            rn = min(32, basis - r0)
            self.groups.append((r0, rn))
            r0 += rn
        self.chunks = []
        c0 = 0
        while c0 < self.width:
            cn = min(2 * elements, self.width - c0)
            self.chunks.append((c0, cn))
            c0 += cn

    def var(self, v):
        return slice(v * self.elements, (v + 1) * self.elements)


def fill_left(n, left, left_f32, pad, project, mats):
    pad[...] = jnp.zeros_like(pad)
    for m in range(n.fbasis):
        for g in range(4):
            r = g * n.mp + m
            pad[r : r + 1, : n.basis] = project[m, g : g + 1, :]
    for d in range(3):
        r = n.fm + d * n.basis
        pad[r : r + n.basis, : n.basis] = mats[d]
    w = pad[...]
    hi = w.astype(BF16).astype(F32)
    lo = w - hi
    left[:, :LANES] = (hi + pltpu.roll(lo, KB, 1)).astype(BF16)
    left[:, LANES : LANES + KB] = hi[:, :KB].astype(BF16)


def put(n, right, r0, v, x):
    rows = x.shape[0]
    if rows % 16:
        x = jnp.concatenate([x, jnp.zeros((16 - rows % 16, x.shape[1]), F32)], axis=0)
        rows = x.shape[0]
    hi, lo = halves(x)
    c = n.var(v)
    right[r0 : r0 + rows, c] = hi
    right[KB + r0 : KB + r0 + rows, c] = hi
    right[2 * KB + r0 : 2 * KB + r0 + rows, c] = lo


def mix(n, load, terms, coef):
    acc = [None] * n.nvar
    for v in range(n.nvar):
        for k in range(terms):
            t = load(v, k)
            for w in range(n.nvar):
                p = t * coef(v, w, k)
                acc[w] = p if acc[w] is None else acc[w] + p
    return acc


def spread_all(n, spread, left, right, lo_row):
    for c0, cn in n.chunks:
        spread[lo_row:, c0 : c0 + cn] = dot(left[lo_row:, :], right[:, c0 : c0 + cn])


def star_mix(n, spread, star, r0, rn):
    def load(v, d):
        r = n.fm + d * n.basis + r0
        return spread[r : r + rn, n.var(v)]

    return mix(n, load, 3, lambda v, w, d: star[v, w, d : d + 1, :])


def predict(n, left, right, spread, star, sums, weights):
    def body(k, carry):
        inv, two = carry
        kf = (k + 1).astype(F32)
        inv = inv / kf
        two = two * 2.0
        spread_all(n, spread, left, right, n.fm)
        scale = weights(inv, two)
        for r0, rn in n.groups:
            acc = star_mix(n, spread, star, r0, rn)
            for w in range(n.nvar):
                c = n.var(w)
                for field, s in zip(sums, scale):
                    field[r0 : r0 + rn, c] += s * acc[w]
                put(n, right, r0, w, acc[w])
        return inv, two

    lax.fori_loop(1, TAYLOR_TERMS, body, (jnp.float32(1.0), jnp.float32(2.0)))


def fill_right(n, right, field):
    for r0, rn in n.groups:
        for v in range(n.nvar):
            put(n, right, r0, v, field[r0 : r0 + rn, n.var(v)])


def send_onehot(n, onehot, keys, send_element, send_face):
    keys[...] = jnp.full(keys.shape, -1, jnp.int32)
    keys[0:1, : n.slots] = send_face[...] * n.elements + send_element[...]
    row = lax.broadcasted_iota(jnp.int32, onehot.shape, 0)
    onehot[...] = jnp.where(row == keys[0:1, :], 1.0, 0.0).astype(BF16)


def traces_and_sends(n, left, right, table, onehot, turned, lower, upper, peers):
    for v in range(n.nvar):
        p = dot(left[: n.fm, :], right[:, n.var(v)])
        for g in range(4):
            table[v * n.mp : (v + 1) * n.mp, n.var(g)] = p[g * n.mp : (g + 1) * n.mp]
    hi, lo = halves(table[...])
    chosen = dot(hi, onehot[...]) + dot(lo, onehot[...])
    curve = chosen[:, :LANES]
    first, rest = curve[: n.half], curve[n.half :]
    short = n.half - rest.shape[0]
    if short:
        rest = jnp.concatenate([rest, jnp.zeros((short, LANES), F32)], axis=0)
    lane = lax.broadcasted_iota(jnp.int32, first.shape, 1)
    lower[...] = jnp.where(lane < HALO_CURVE, first, pltpu.roll(rest, HALO_CURVE, 1))
    upper[...] = jnp.where(lane < HALO_CURVE, pltpu.roll(first, HALO_CURVE, 1), rest)
    turned[...] = jnp.zeros_like(turned)
    wide = jnp.concatenate([chosen[:, LANES:], jnp.zeros((n.rows_pad - n.rows, n.slot_cols - LANES), F32)], axis=0)
    turned[...] = wide.T
    here = lax.axis_index("sub")
    for k, ref in enumerate(peers):
        block = lax.rem(here + k, n.subs)
        ref[...] = turned[pl.ds(pl.multiple_of(block * HALO_PEER, HALO_PEER), HALO_PEER), :]


def first_kernel(n, dof, project, stiffness, star, send_element, send_face,
                 first, second, table, lower, upper, *rest):
    peers = rest[: n.subs]
    left, onehot, right, spread, pad, keys, turned = rest[n.subs :]
    fill_left(n, left, None, pad, project, [stiffness[d].T for d in range(3)])
    send_onehot(n, onehot, keys, send_element, send_face)
    for v in range(n.nvar):
        x = dof[v]
        first[:, n.var(v)] = x
        second[:, n.var(v)] = x
    fill_right(n, right, first)
    predict(n, left, right, spread, star, [first, second],
            lambda inv, two: [inv, (two - 1.0) * inv])
    fill_right(n, right, first)
    traces_and_sends(n, left, right, table, onehot, turned, lower, upper, peers)


def own_part(n, left, right, spread, star, flux_local, lift, solved, stacked, part):
    spread_all(n, spread, left, right, 0)
    for g in range(4):
        def load(v, k, g=g):
            return spread[g * n.mp : (g + 1) * n.mp, n.var(v)]

        acc = mix(n, load, 1, lambda v, w, k, g=g: flux_local[v, w, g : g + 1, :])
        for w in range(n.nvar):
            solved[g * n.mp : (g + 1) * n.mp, n.var(w)] = acc[w]
    for w in range(n.nvar):
        hi, lo = halves(solved[:, n.var(w)])
        stacked[: n.fm, n.var(w)] = hi
        stacked[LANES : LANES + n.fm, n.var(w)] = lo
    stacked[n.fm : LANES, :] = jnp.zeros((LANES - n.fm, n.width), BF16)
    stacked[LANES + n.fm :, :] = jnp.zeros((LANES - n.fm, n.width), BF16)
    for r0, rn in n.groups:
        acc = star_mix(n, spread, star, r0, rn)
        for w in range(n.nvar):
            part[r0 : r0 + rn, n.var(w)] = acc[w]
    for c0, cn in n.chunks:
        out = dot(lift[...], stacked[:, c0 : c0 + cn])
        part[:, c0 : c0 + cn] = part[:, c0 : c0 + cn] - (out[: n.basis] + out[n.basis :])


def lift_rows(n, out, tall, w):
    hi = w.astype(BF16).astype(F32)
    lo = w - hi
    span = w.shape[1]
    tall[: n.basis, :span] = hi
    tall[n.basis : 2 * n.basis, :span] = lo
    out[:, :span] = tall[: 2 * n.basis, :span].astype(BF16)
    tall[n.basis : 2 * n.basis, :span] = jnp.zeros_like(lo)
    out[:, span:] = tall[: 2 * n.basis, :span].astype(BF16)


def second_kernel(n, field, table, project, stiffness, star, face_lift, face_rotate, flux_local, index, face, orient,
                  part, found, left, lift, lift_turned, onehot_own, onehot_halo, masks,
                  right, spread, pad, solved, stacked, wide, tall, square, mask_rows):
    fill_left(n, left, None, pad, project, [stiffness[d] for d in range(3)])
    fill_right(n, right, field)
    wide[...] = jnp.zeros_like(wide)
    square[...] = jnp.zeros_like(square)
    for m in range(n.fbasis):
        for g in range(4):
            r = g * n.mp + m
            square[r : r + 1, : n.basis] = face_lift[m, g : g + 1, :]
    base = square[...]
    lift_rows(n, lift, tall, base.T[: n.basis, :])
    for o in range(3):
        square[...] = jnp.zeros_like(square)
        square[: n.fbasis, : n.fbasis] = face_rotate[o]
        turn = square[...].T[: n.mp, :]
        turn = turn[:, : n.mp]
        for g in range(4):
            r = o * n.fm + g * n.mp
            wide[r : r + n.mp, :] = jnp.dot(turn, base[g * n.mp : (g + 1) * n.mp, :],
                                            precision=lax.Precision.HIGHEST, preferred_element_type=F32)
    blocks = wide.shape[0] // LANES
    turned = jnp.concatenate([wide[i * LANES : (i + 1) * LANES, :].T[: n.basis, :] for i in range(blocks)], axis=1)
    lift_rows(n, lift_turned, tall, turned)
    dom = lax.axis_index("dom")
    last = lax.axis_size("dom") - 1
    for f in range(4):
        idx = index[f : f + 1, :]
        slot = idx - n.elements
        own = jnp.where(slot < 0, face[f : f + 1, :] * n.elements + idx, -1)
        slot = jnp.where(jnp.logical_and(slot < HALO_CURVE, dom == 0), -1, slot)
        high = jnp.logical_and(slot >= HALO_CURVE, slot < 2 * HALO_CURVE)
        slot = jnp.where(jnp.logical_and(high, dom == last), -1, slot)
        row = lax.broadcasted_iota(jnp.int32, (n.cols4, n.elements), 0)
        onehot_own[:, n.var(f)] = jnp.where(row == own, 1.0, 0.0).astype(BF16)
        row = lax.broadcasted_iota(jnp.int32, (n.slot_cols, n.elements), 0)
        onehot_halo[:, n.var(f)] = jnp.where(row == slot, 1.0, 0.0).astype(BF16)
        for o in range(3):
            r = o * n.fm + f * n.mp
            mask_rows[r : r + n.mp, :] = jnp.broadcast_to(
                jnp.where(orient[f : f + 1, :] == o, 1.0, 0.0), (n.mp, n.elements))
    masks[...] = mask_rows[...].astype(BF16)
    own_part(n, left, right, spread, star, flux_local, lift, solved, stacked, part)
    hi, lo = halves(table[...])
    found[...] = dot(hi, onehot_own[...]) + dot(lo, onehot_own[...])


def neighbour_part(n, below, above, peers, found, onehot_halo, flux_neighbour, masks, lift_turned,
                   traces, solved, stacked, turned):
    lane = lax.broadcasted_iota(jnp.int32, below.shape, 1)
    b, a = below[...], above[...]
    first = jnp.where(lane < HALO_CURVE, b, pltpu.roll(a, HALO_CURVE, 1))
    rest = jnp.where(lane < HALO_CURVE, pltpu.roll(b, HALO_CURVE, 1), a)
    curve = jnp.concatenate([first, rest], axis=0)[: n.rows]
    turned[...] = jnp.zeros_like(turned)
    here = lax.axis_index("sub")
    for k, ref in enumerate(peers):
        block = lax.rem(here + n.subs - k, n.subs)
        turned[pl.ds(pl.multiple_of(block * HALO_PEER, HALO_PEER), HALO_PEER), :] = ref[...]
    flat = turned[...].T[: n.rows, :]
    hi, lo = halves(jnp.concatenate([curve, flat], axis=1))
    traces[...] = found[...] + dot(hi, onehot_halo[...]) + dot(lo, onehot_halo[...])
    for f in range(4):
        def load(v, k, f=f):
            return traces[v * n.mp : (v + 1) * n.mp, n.var(f)]

        acc = mix(n, load, 1, lambda v, w, k, f=f: flux_neighbour[v, w, f : f + 1, :])
        for w in range(n.nvar):
            solved[f * n.mp : (f + 1) * n.mp, n.var(w)] = acc[w]
    span = stacked.shape[0] // 2
    for w in range(n.nvar):
        hi, lo = halves(solved[:, n.var(w)])
        for o in range(3):
            m = masks[o * n.fm : (o + 1) * n.fm, :]
            stacked[o * n.fm : (o + 1) * n.fm, n.var(w)] = hi * m
            stacked[span + o * n.fm : span + (o + 1) * n.fm, n.var(w)] = lo * m
    gap = span - 3 * n.fm
    if gap:
        stacked[3 * n.fm : span, :] = jnp.zeros((gap, n.width), BF16)
        stacked[span + 3 * n.fm :, :] = jnp.zeros((gap, n.width), BF16)


def third_kernel(n, *refs):
    below, above = refs[:2]
    peers = refs[2 : 2 + n.subs]
    (found, onehot_halo, flux_neighbour, masks, lift_turned, part, dof, labels, second, star, left, send_onehot_ref,
     later, middle, traces, table, lower, upper) = refs[2 + n.subs : 20 + n.subs]
    sent = refs[20 + n.subs : 20 + 2 * n.subs]
    right, spread, solved, stacked, turned = refs[20 + 2 * n.subs :]
    neighbour_part(n, below, above, peers, found, onehot_halo, flux_neighbour, masks, lift_turned,
                   traces, solved, stacked, turned)
    fine = labels[...] == 0
    for c0, cn in n.chunks:
        out = dot(lift_turned[...], stacked[:, c0 : c0 + cn])
        nb = out[: n.basis] + out[n.basis :]
        for v in range(c0 // n.elements, (c0 + cn) // n.elements):
            c = n.var(v)
            o = v * n.elements - c0
            x = dof[v]
            mid = jnp.where(fine, x + (part[:, c] - nb[:, o : o + n.elements]), x)
            middle[:, c] = mid
            later[:, c] = mid
    fill_right(n, right, middle)
    predict(n, left, right, spread, star, [later], lambda inv, two: [inv])
    for v in range(n.nvar):
        c = n.var(v)
        later[:, c] = jnp.where(fine, later[:, c], second[:, c])
    fill_right(n, right, later)
    traces_and_sends(n, left, right, table, send_onehot_ref, turned, lower, upper, sent)


def fourth_kernel(n, first, second, later, middle, labels, star, left, flux_local, lift, table, onehot_own, traces,
                  part, found, right, spread, solved, stacked):
    fine = labels[...] == 0
    for r0, rn in n.groups:
        for v in range(n.nvar):
            c = n.var(v)
            rows = slice(r0, r0 + rn)
            put(n, right, r0, v, jnp.where(fine, later[rows, c], first[rows, c] + second[rows, c]))
    own_part(n, left, right, spread, star, flux_local, lift, solved, stacked, part)
    part[...] = middle[...] + part[...]
    hi, lo = halves(table[...])
    got = dot(hi, onehot_own[...]) + dot(lo, onehot_own[...])
    for f in range(4):
        c = n.var(f)
        found[:, c] = got[:, c] + jnp.where(fine, 0.0, traces[:, c])


def fifth_kernel(n, *refs):
    below, above = refs[:2]
    peers = refs[2 : 2 + n.subs]
    found, onehot_halo, flux_neighbour, masks, lift_turned, part, out, traces, solved, stacked, turned = refs[2 + n.subs :]
    neighbour_part(n, below, above, peers, found, onehot_halo, flux_neighbour, masks, lift_turned,
                   traces, solved, stacked, turned)
    for c0, cn in n.chunks:
        got = dot(lift_turned[...], stacked[:, c0 : c0 + cn])
        nb = got[: n.basis] + got[n.basis :]
        for v in range(c0 // n.elements, (c0 + cn) // n.elements):
            o = v * n.elements - c0
            out[v] = part[:, n.var(v)] - nb[:, o : o + n.elements]


def call(kernel, n, operands, outs, scratch, name):
    vm = pl.BlockSpec(memory_space=pltpu.VMEM)

    def body(*refs):
        kernel(n, *refs)

    return pl.pallas_call(
        body,
        out_shape=[jax.ShapeDtypeStruct(s, t) for s, t in outs],
        in_specs=[vm] * len(operands),
        out_specs=[vm] * len(outs),
        scratch_shapes=[pltpu.VMEM(s, t) for s, t in scratch],
        name=name,
    )(*operands)


def ring(value, axis, by):
    peers = lax.axis_size(axis)
    return lax.ppermute(value, axis, [(i, (i + by) % peers) for i in range(peers)])


def exchange(lower, upper, peers):
    below = ring(upper, "dom", 1)
    above = ring(lower, "dom", -1)
    return [below, above, peers[0]] + [ring(p, "sub", k) for k, p in enumerate(peers) if k]


def per_device(dof_values, stiffness, face_project, face_lift, face_rotate, star_matrices, flux_local, flux_neighbour,
               cluster_labels, neighbour_index, neighbour_face, neighbour_orient, send_element, send_face):
    n = Dims(dof_values.shape[0], dof_values.shape[1], dof_values.shape[2], face_project.shape[1],
             send_element.shape[1], lax.axis_size("sub"))
    dof = jnp.transpose(dof_values, (1, 0, 2))
    star = jnp.transpose(star_matrices, (1, 2, 0, 3))
    local = jnp.transpose(flux_local, (1, 2, 0, 3))
    remote = jnp.transpose(flux_neighbour, (1, 2, 0, 3))
    project = jnp.transpose(face_project, (1, 0, 2))
    lift = jnp.transpose(face_lift, (2, 0, 1))
    labels = cluster_labels.reshape(1, n.elements)

    field = ((n.basis, n.width), F32)
    grid = ((n.rows, n.cols4), F32)
    pack = ((n.half, LANES), F32)
    peer = ((HALO_PEER, n.rows_pad), F32)
    left_t = ((n.left_rows, 3 * KB), BF16)
    right_t = ((3 * KB, n.width), BF16)
    spread_t = ((n.left_rows, n.width), F32)
    turned_t = ((n.slot_cols - LANES, n.rows_pad), F32)
    solved_t = ((n.fm, n.width), F32)
    own_stack = ((2 * LANES, n.width), BF16)
    rot_rows = up(3 * n.fm, LANES)
    rot_stack = ((2 * rot_rows, n.width), BF16)
    pad_t = ((n.left_rows, LANES), F32)

    outs = call(
        first_kernel, n, [dof, project, stiffness, star, send_element, send_face],
        [field, field, grid, pack, pack] + [peer] * n.subs + [left_t, ((n.cols4, n.slot_cols), BF16)],
        [right_t, spread_t, pad_t, ((8, n.slot_cols), jnp.int32), turned_t], "predict_first")
    first, second, table, lower, upper = outs[:5]
    peers = outs[5 : 5 + n.subs]
    left_one, send_sel = outs[5 + n.subs :]
    got = exchange(lower, upper, peers)
    part, found, left_two, lift_own, lift_rot, sel_own, sel_halo, masks = call(
        second_kernel, n,
        [first, table, project, stiffness, star, lift, face_rotate, local, neighbour_index, neighbour_face, neighbour_orient],
        [field, grid, left_t, ((2 * n.basis, 2 * LANES), BF16), ((2 * n.basis, 2 * rot_rows), BF16),
         ((n.cols4, n.cols4), BF16), ((n.slot_cols, n.cols4), BF16), ((3 * n.fm, n.elements), BF16)],
        [right_t, spread_t, pad_t, solved_t, own_stack, ((rot_rows, LANES), F32), ((2 * n.basis, rot_rows), F32),
         ((LANES, LANES), F32), ((3 * n.fm, n.elements), F32)], "own_first")
    outs = call(
        third_kernel, n,
        got + [found, sel_halo, remote, masks, lift_rot, part, dof, labels, second, star, left_one, send_sel],
        [field, field, grid, grid, pack, pack] + [peer] * n.subs,
        [right_t, spread_t, solved_t, rot_stack, turned_t], "neighbour_first")
    later, middle, traces, table, lower, upper = outs[:6]
    got = exchange(lower, upper, outs[6:])
    part, found = call(
        fourth_kernel, n,
        [first, second, later, middle, labels, star, left_two, local, lift_own, table, sel_own, traces],
        [field, grid], [right_t, spread_t, solved_t, own_stack], "own_second")
    (out,) = call(
        fifth_kernel, n, got + [found, sel_halo, remote, masks, lift_rot, part],
        [((n.nvar, n.basis, n.elements), F32)], [grid, solved_t, rot_stack, turned_t], "neighbour_second")
    return jnp.transpose(out, (1, 0, 2))


def solution(mesh):
    cells = ("dom", "sub")
    in_specs = (
        P(None, None, cells),
        P(),
        P(),
        P(),
        P(),
        P(None, None, None, cells),
        P(None, None, None, cells),
        P(None, None, None, cells),
        P(cells),
        P(None, cells),
        P(None, cells),
        P(None, cells),
        P(cells, None),
        P(cells, None),
    )
    out_specs = P(None, None, cells)
    return jax.shard_map(per_device, mesh=mesh, in_specs=in_specs, out_specs=out_specs, check_vma=False)
```

profile of v0, /device:TPU:0, one launch (start us, length us, event | category | flops | bytes accessed | tf_op | source)
XLA Modules:
  0.0 45.2 jit_solution(14868914955743115893)
XLA Ops:
  0.0 7.1 %predict_first.1 = (f32[56,1152]{1,0:T(8,128)}, f32[56,1152]{1,0:T(8,128)}, f32[216,512]{1,0:T(8,128)}, f32[112,128]{1,0:T(8,128)}, f32[112,128]{1,0:T(8,128)}, ...) custom-call(f32[9,56,128]{2,1,0:T(8,128)} %bitcast.12, ...), custom_call_target="tpu_custom_call" | custom-call | tf_op jit(solution)/shard_map/predict_first/pallas_call | solution.py:370
  7.1 0.0 copy-start.11
  7.1 0.5 %collective-permute-start = (f32[112,128]{1,0:T(8,128)}, f32[112,128]{1,0:T(8,128)S(1)}, u32[]{:S(2)}, u32[]{:S(2)}) collective-permute-start(f32[112,128]{1,0:T(8,128)} %get-tuple-element.36), channel_id=1, source_target_pairs={{0,4},{4,8},{8,12},{12,16},{16,20},{20,24},{24,28},{28,0},{1,5},{5... | collective-permute-start | bytes 172040 | tf_op jit(solution)/shard_map/ppermute | solution.py:382
  7.6 2.9 %collective-permute-start.1 = (f32[112,128]{1,0:T(8,128)}, f32[112,128]{1,0:T(8,128)S(1)}, u32[]{:S(2)}, u32[]{:S(2)}) collective-permute-start(f32[112,128]{1,0:T(8,128)} %get-tuple-element.37), channel_id=1, source_target_pairs={{0,28},{4,0},{8,4},{12,8},{16,12},{20,16},{24,20},{28,24},{1,29},{... | collective-permute-start | bytes 172040 | tf_op jit(solution)/shard_map/ppermute | solution.py:382
  10.6 2.3 %collective-permute-start.2 = (f32[8,256]{1,0:T(8,128)}, f32[8,256]{1,0:T(8,128)S(1)}, u32[]{:S(2)}, u32[]{:S(2)}) collective-permute-start(f32[8,256]{1,0:T(8,128)} %get-tuple-element.39), channel_id=1, source_target_pairs={{0,1},{1,2},{2,3},{3,0},{4,5},{5,6},{6,7},{7,4},{8,9},{9,10},{10,1... | collective-permute-start | bytes 24584 | tf_op jit(solution)/shard_map/ppermute | solution.py:382
  12.9 2.6 %collective-permute-start.3 = (f32[8,256]{1,0:T(8,128)}, f32[8,256]{1,0:T(8,128)S(1)}, u32[]{:S(2)}, u32[]{:S(2)}) collective-permute-start(f32[8,256]{1,0:T(8,128)} %get-tuple-element.40), channel_id=1, source_target_pairs={{0,2},{1,3},{2,0},{3,1},{4,6},{5,7},{6,4},{7,5},{8,10},{9,11},{10,... | collective-permute-start | bytes 24584 | tf_op jit(solution)/shard_map/ppermute | solution.py:382
  15.4 0.0 copy-done.11
  15.4 1.3 %collective-permute-start.4 = (f32[8,256]{1,0:T(8,128)S(1)}, f32[8,256]{1,0:T(8,128)S(1)}, u32[]{:S(2)}, u32[]{:S(2)}) collective-permute-start(f32[8,256]{1,0:T(8,128)S(1)} %copy-done.11), channel_id=1, source_target_pairs={{0,3},{1,0},{2,1},{3,2},{4,7},{5,4},{6,5},{7,6},{8,11},{9,8},{10,9... | collective-permute-start | bytes 24584 | tf_op jit(solution)/shard_map/ppermute | solution.py:382
  16.8 4.4 %own_first.1 = (f32[56,1152]{1,0:T(8,128)}, f32[216,512]{1,0:T(8,128)}, bf16[264,192]{1,0:T(8,128)(2,1)}, bf16[112,256]{1,0:T(8,128)(2,1)}, bf16[112,768]{1,0:T(...) custom-call(f32[56,1152]{1,0:T(8,128)} %get-tuple-element.42.refs_0_, ...), custom_call_target="tpu_custom_call" | custom-call | tf_op jit(solution)/shard_map/own_first/pallas_call | solution.py:370
  21.1 0.0 collective-permute-done.2.refs_3_
  21.2 0.0 copy-start.4
  21.2 0.0 collective-permute-done.3.refs_4_
  21.2 0.0 copy-start.5
  21.2 0.0 collective-permute-done.4.refs_5_
  21.2 0.0 copy-start.7
  21.2 0.0 collective-permute-done.refs_0_
  21.2 0.0 copy-start
  21.2 0.0 collective-permute-done.1.refs_1_
  21.2 0.0 copy-start.1
  21.3 0.5 %copy-done.4 = f32[8,256]{1,0:T(8,128)} copy-done((f32[8,256]{1,0:T(8,128)}, f32[8,256]{1,0:T(8,128)S(1)}, u32[]{:S(2)}) %copy-start.4) | copy-done | bytes 8216
  21.8 0.0 copy-done.5
  21.8 0.0 copy-done.7
  21.8 0.0 copy-done
  21.8 0.0 copy-done.1
  21.9 8.5 %neighbour_first.1 = (f32[56,1152]{1,0:T(8,128)}, f32[56,1152]{1,0:T(8,128)}, f32[216,512]{1,0:T(8,128)}, f32[216,512]{1,0:T(8,128)}, f32[112,128]{1,0:T(8,128)}...) custom-call(f32[112,128]{1,0:T(8,128)} %copy-done, ...), custom_call_target="tpu_custom_call" | custom-call | tf_op jit(solution)/shard_map/neighbour_first/pallas_call | solution.py:370
  30.4 0.0 copy-start.10
  30.4 0.1 collective-permute-start.5
  30.5 2.6 %collective-permute-start.6 = (f32[112,128]{1,0:T(8,128)}, f32[112,128]{1,0:T(8,128)S(1)}, u32[]{:S(2)}, u32[]{:S(2)}) collective-permute-start(f32[112,128]{1,0:T(8,128)} %get-tuple-element.53), channel_id=1, source_target_pairs={{0,28},{4,0},{8,4},{12,8},{16,12},{20,16},{24,20},{28,24},{1,29},{... | collective-permute-start | bytes 172040 | tf_op jit(solution)/shard_map/ppermute | solution.py:382
  33.1 0.7 %collective-permute-start.7 = (f32[8,256]{1,0:T(8,128)}, f32[8,256]{1,0:T(8,128)S(1)}, u32[]{:S(2)}, u32[]{:S(2)}) collective-permute-start(f32[8,256]{1,0:T(8,128)} %get-tuple-element.55), channel_id=1, source_target_pairs={{0,1},{1,2},{2,3},{3,0},{4,5},{5,6},{6,7},{7,4},{8,9},{9,10},{10,1... | collective-permute-start | bytes 24584 | tf_op jit(solution)/shard_map/ppermute | solution.py:382
  33.8 0.9 %collective-permute-start.8 = (f32[8,256]{1,0:T(8,128)}, f32[8,256]{1,0:T(8,128)S(1)}, u32[]{:S(2)}, u32[]{:S(2)}) collective-permute-start(f32[8,256]{1,0:T(8,128)} %get-tuple-element.56), channel_id=1, source_target_pairs={{0,2},{1,3},{2,0},{3,1},{4,6},{5,7},{6,4},{7,5},{8,10},{9,11},{10,... | collective-permute-start | bytes 24584 | tf_op jit(solution)/shard_map/ppermute | solution.py:382
  34.7 0.0 copy-done.10
  34.7 2.2 %collective-permute-start.9 = (f32[8,256]{1,0:T(8,128)S(1)}, f32[8,256]{1,0:T(8,128)S(1)}, u32[]{:S(2)}, u32[]{:S(2)}) collective-permute-start(f32[8,256]{1,0:T(8,128)S(1)} %copy-done.10), channel_id=1, source_target_pairs={{0,3},{1,0},{2,1},{3,2},{4,7},{5,4},{6,5},{7,6},{8,11},{9,8},{10,9... | collective-permute-start | bytes 24584 | tf_op jit(solution)/shard_map/ppermute | solution.py:382
  36.9 4.2 %own_second.1 = (f32[56,1152]{1,0:T(8,128)}, f32[216,512]{1,0:T(8,128)}) custom-call(f32[56,1152]{1,0:T(8,128)} %get-tuple-element.42.refs_0_, f32[56,1152]{1,0:T(8,128)} %get-tuple-element.49.refs_14_.refs_1_, f32[56,1152]{1,0:T(8,128)} %get-tuple-element.58.refs_2_, f32[56,1152]{1,0:T(8,128)} %get-tuple-element.59.refs_3_, s32[1,128]{1,0:T(1,128)} %bitcast.22, ...), custom_call_target="tpu_custom_call" | custom-call | tf_op jit(solution)/shard_map/own_second/pallas_call | solution.py:370
  41.2 0.0 collective-permute-done.7.refs_3_
  41.2 0.0 collective-permute-done.8.refs_4_
  41.2 0.0 copy-start.8
  41.2 0.0 collective-permute-done.9.refs_5_
  41.2 0.0 copy-start.9
  41.2 0.0 collective-permute-done.5.refs_0_
  41.2 0.0 copy-start.2
  41.2 0.0 collective-permute-done.6.refs_1_
  41.3 0.0 copy-start.3
  41.3 0.5 %copy-done.6 = f32[8,256]{1,0:T(8,128)} copy-done((f32[8,256]{1,0:T(8,128)}, f32[8,256]{1,0:T(8,128)S(1)}, u32[]{:S(2)}) %copy-start.6) | copy-done | bytes 8216
  41.8 0.0 copy-done.8
  41.8 0.0 copy-done.9
  41.8 0.0 copy-done.2
  41.9 0.0 copy-done.3
  41.9 3.3 %neighbour_second.1 = f32[9,56,128]{2,1,0:T(8,128)} custom-call(f32[112,128]{1,0:T(8,128)} %copy-done.2, f32[112,128]{1,0:T(8,128)} %copy-done.3, f32[8,256]{1,0:T(8,128)} %get-tuple-element.54.refs_2_, f32[8,256]{1,0:T(8,128)} %copy-done.6, f32[8,256]{1,0:T(8,128)} %copy-done.8, f32[8,256]{1,0:T(8,128)} %copy-done.9, f32[216,512]{1,0:T(8,128)} %get-tuple-element.65.refs_6_, ...), custom_call_target="tpu_custom_call" | custom-call | tf_op jit(solution)/shard_map/neighbour_second/pallas_call | solution.py:370
  (1 shorter events, 0.0 us)
Async XLA Ops:
  7.1 8.4 %copy-start.11 = (f32[8,256]{1,0:T(8,128)S(1)}, f32[8,256]{1,0:T(8,128)}, u32[]{:S(2)}) copy-start(f32[8,256]{1,0:T(8,128)} %get-tuple-element.41) | copy-start | bytes 24580
  7.1 14.1 %collective-permute-start = (f32[112,128]{1,0:T(8,128)}, f32[112,128]{1,0:T(8,128)S(1)}, u32[]{:S(2)}, u32[]{:S(2)}) collective-permute-start(f32[112,128]{1,0:T(8,128)} %get-tuple-element.36), channel_id=1, source_target_pairs={{0,4},{4,8},{8,12},{12,16},{16,20},{20,24},{24,28},{28,0},{1,5},{5... | collective-permute-start | bytes 172040 | tf_op jit(solution)/shard_map/ppermute | solution.py:382
  7.6 13.6 %collective-permute-start.1 = (f32[112,128]{1,0:T(8,128)}, f32[112,128]{1,0:T(8,128)S(1)}, u32[]{:S(2)}, u32[]{:S(2)}) collective-permute-start(f32[112,128]{1,0:T(8,128)} %get-tuple-element.37), channel_id=1, source_target_pairs={{0,28},{4,0},{8,4},{12,8},{16,12},{20,16},{24,20},{28,24},{1,29},{... | collective-permute-start | bytes 172040 | tf_op jit(solution)/shard_map/ppermute | solution.py:382
  10.6 10.6 %collective-permute-start.2 = (f32[8,256]{1,0:T(8,128)}, f32[8,256]{1,0:T(8,128)S(1)}, u32[]{:S(2)}, u32[]{:S(2)}) collective-permute-start(f32[8,256]{1,0:T(8,128)} %get-tuple-element.39), channel_id=1, source_target_pairs={{0,1},{1,2},{2,3},{3,0},{4,5},{5,6},{6,7},{7,4},{8,9},{9,10},{10,1... | collective-permute-start | bytes 24584 | tf_op jit(solution)/shard_map/ppermute | solution.py:382
  12.9 8.3 %collective-permute-start.3 = (f32[8,256]{1,0:T(8,128)}, f32[8,256]{1,0:T(8,128)S(1)}, u32[]{:S(2)}, u32[]{:S(2)}) collective-permute-start(f32[8,256]{1,0:T(8,128)} %get-tuple-element.40), channel_id=1, source_target_pairs={{0,2},{1,3},{2,0},{3,1},{4,6},{5,7},{6,4},{7,5},{8,10},{9,11},{10,... | collective-permute-start | bytes 24584 | tf_op jit(solution)/shard_map/ppermute | solution.py:382
  15.4 5.7 %collective-permute-start.4 = (f32[8,256]{1,0:T(8,128)S(1)}, f32[8,256]{1,0:T(8,128)S(1)}, u32[]{:S(2)}, u32[]{:S(2)}) collective-permute-start(f32[8,256]{1,0:T(8,128)S(1)} %copy-done.11), channel_id=1, source_target_pairs={{0,3},{1,0},{2,1},{3,2},{4,7},{5,4},{6,5},{7,6},{8,11},{9,8},{10,9... | collective-permute-start | bytes 24584 | tf_op jit(solution)/shard_map/ppermute | solution.py:382
  21.2 0.6 %copy-start.4 = (f32[8,256]{1,0:T(8,128)}, f32[8,256]{1,0:T(8,128)S(1)}, u32[]{:S(2)}) copy-start(f32[8,256]{1,0:T(8,128)S(1)} %collective-permute-done.2.refs_3_) | copy-start | bytes 24580
  21.2 0.6 %copy-start.5 = (f32[8,256]{1,0:T(8,128)}, f32[8,256]{1,0:T(8,128)S(1)}, u32[]{:S(2)}) copy-start(f32[8,256]{1,0:T(8,128)S(1)} %collective-permute-done.3.refs_4_) | copy-start | bytes 24580
  21.2 0.6 %copy-start.7 = (f32[8,256]{1,0:T(8,128)}, f32[8,256]{1,0:T(8,128)S(1)}, u32[]{:S(2)}) copy-start(f32[8,256]{1,0:T(8,128)S(1)} %collective-permute-done.4.refs_5_) | copy-start | bytes 24580
  21.2 0.6 %copy-start = (f32[112,128]{1,0:T(8,128)}, f32[112,128]{1,0:T(8,128)S(1)}, u32[]{:S(2)}) copy-start(f32[112,128]{1,0:T(8,128)S(1)} %collective-permute-done.refs_0_) | copy-start | bytes 172036
  21.2 0.6 %copy-start.1 = (f32[112,128]{1,0:T(8,128)}, f32[112,128]{1,0:T(8,128)S(1)}, u32[]{:S(2)}) copy-start(f32[112,128]{1,0:T(8,128)S(1)} %collective-permute-done.1.refs_1_) | copy-start | bytes 172036
  30.4 4.3 %copy-start.10 = (f32[8,256]{1,0:T(8,128)S(1)}, f32[8,256]{1,0:T(8,128)}, u32[]{:S(2)}) copy-start(f32[8,256]{1,0:T(8,128)} %get-tuple-element.57) | copy-start | bytes 24580
  30.4 10.8 %collective-permute-start.5 = (f32[112,128]{1,0:T(8,128)}, f32[112,128]{1,0:T(8,128)S(1)}, u32[]{:S(2)}, u32[]{:S(2)}) collective-permute-start(f32[112,128]{1,0:T(8,128)} %get-tuple-element.52), channel_id=1, source_target_pairs={{0,4},{4,8},{8,12},{12,16},{16,20},{20,24},{24,28},{28,0},{1,5},{5... | collective-permute-start | bytes 172040 | tf_op jit(solution)/shard_map/ppermute | solution.py:382
  30.5 10.8 %collective-permute-start.6 = (f32[112,128]{1,0:T(8,128)}, f32[112,128]{1,0:T(8,128)S(1)}, u32[]{:S(2)}, u32[]{:S(2)}) collective-permute-start(f32[112,128]{1,0:T(8,128)} %get-tuple-element.53), channel_id=1, source_target_pairs={{0,28},{4,0},{8,4},{12,8},{16,12},{20,16},{24,20},{28,24},{1,29},{... | collective-permute-start | bytes 172040 | tf_op jit(solution)/shard_map/ppermute | solution.py:382
  33.1 8.1 %collective-permute-start.7 = (f32[8,256]{1,0:T(8,128)}, f32[8,256]{1,0:T(8,128)S(1)}, u32[]{:S(2)}, u32[]{:S(2)}) collective-permute-start(f32[8,256]{1,0:T(8,128)} %get-tuple-element.55), channel_id=1, source_target_pairs={{0,1},{1,2},{2,3},{3,0},{4,5},{5,6},{6,7},{7,4},{8,9},{9,10},{10,1... | collective-permute-start | bytes 24584 | tf_op jit(solution)/shard_map/ppermute | solution.py:382
  33.8 7.4 %collective-permute-start.8 = (f32[8,256]{1,0:T(8,128)}, f32[8,256]{1,0:T(8,128)S(1)}, u32[]{:S(2)}, u32[]{:S(2)}) collective-permute-start(f32[8,256]{1,0:T(8,128)} %get-tuple-element.56), channel_id=1, source_target_pairs={{0,2},{1,3},{2,0},{3,1},{4,6},{5,7},{6,4},{7,5},{8,10},{9,11},{10,... | collective-permute-start | bytes 24584 | tf_op jit(solution)/shard_map/ppermute | solution.py:382
  34.7 6.5 %collective-permute-start.9 = (f32[8,256]{1,0:T(8,128)S(1)}, f32[8,256]{1,0:T(8,128)S(1)}, u32[]{:S(2)}, u32[]{:S(2)}) collective-permute-start(f32[8,256]{1,0:T(8,128)S(1)} %copy-done.10), channel_id=1, source_target_pairs={{0,3},{1,0},{2,1},{3,2},{4,7},{5,4},{6,5},{7,6},{8,11},{9,8},{10,9... | collective-permute-start | bytes 24584 | tf_op jit(solution)/shard_map/ppermute | solution.py:382
  41.2 0.6 %copy-start.6 = (f32[8,256]{1,0:T(8,128)}, f32[8,256]{1,0:T(8,128)S(1)}, u32[]{:S(2)}) copy-start(f32[8,256]{1,0:T(8,128)S(1)} %collective-permute-done.7.refs_3_) | copy-start | bytes 24580
  41.2 0.6 %copy-start.8 = (f32[8,256]{1,0:T(8,128)}, f32[8,256]{1,0:T(8,128)S(1)}, u32[]{:S(2)}) copy-start(f32[8,256]{1,0:T(8,128)S(1)} %collective-permute-done.8.refs_4_) | copy-start | bytes 24580
  41.2 0.6 %copy-start.9 = (f32[8,256]{1,0:T(8,128)}, f32[8,256]{1,0:T(8,128)S(1)}, u32[]{:S(2)}) copy-start(f32[8,256]{1,0:T(8,128)S(1)} %collective-permute-done.9.refs_5_) | copy-start | bytes 24580
  41.2 0.6 %copy-start.2 = (f32[112,128]{1,0:T(8,128)}, f32[112,128]{1,0:T(8,128)S(1)}, u32[]{:S(2)}) copy-start(f32[112,128]{1,0:T(8,128)S(1)} %collective-permute-done.5.refs_0_) | copy-start | bytes 172036
  41.3 0.6 %copy-start.3 = (f32[112,128]{1,0:T(8,128)}, f32[112,128]{1,0:T(8,128)S(1)}, u32[]{:S(2)}) copy-start(f32[112,128]{1,0:T(8,128)S(1)} %collective-permute-done.6.refs_1_) | copy-start | bytes 172036
where the time goes:
time: 45.4 us; the launch traced here: 45.2 us
  Pallas kernels  27.5 us (61%)
  starting transfers between devices  16.2 us (36%)
  local copies, waits for them, and re-layouts  1.27 us (3%)
    pallas_call x5, Pallas kernels, call(): pl.pallas_call(body, out_shape=[jax.ShapeDtypeStruct(s, t) for s, t in ou...  27.5 us
    ppermute x10, starting transfers between devices, ring(): lax.ppermute(value, axis, [(i, (i + by) % peers) for i in range(peers)])  16.2 us
    unnamed x24, local copies, waits for them, and re-layouts  1.27 us
  transfers between devices with their start and end apart: 10, of which 0 were waited for; matrix products, arithmetic and copies ran while one was open for 0% of the time, Pallas kernels for 19%

commit v1 on v0

--- a/solution.py
+++ b/solution.py
@@ -11,6 +11,7 @@
 F32 = jnp.float32
 BF16 = jnp.bfloat16
 LANES = 128
+FAR = 14
 KB = 64
 
 
@@ -142,7 +143,7 @@
     onehot[...] = jnp.where(row == keys[0:1, :], 1.0, 0.0).astype(BF16)
 
 
-def traces_and_sends(n, left, right, table, onehot, turned, lower, upper, peers):
+def traces_and_sends(n, left, right, table, onehot, turned, near, far, peers):
     for v in range(n.nvar):
         p = dot(left[: n.fm, :], right[:, n.var(v)])
         for g in range(4):
@@ -155,32 +156,47 @@
     if short:
         rest = jnp.concatenate([rest, jnp.zeros((short, LANES), F32)], axis=0)
     lane = lax.broadcasted_iota(jnp.int32, first.shape, 1)
-    lower[...] = jnp.where(lane < HALO_CURVE, first, pltpu.roll(rest, HALO_CURVE, 1))
-    upper[...] = jnp.where(lane < HALO_CURVE, pltpu.roll(first, HALO_CURVE, 1), rest)
+    lower = jnp.where(lane < HALO_CURVE, first, pltpu.roll(rest, HALO_CURVE, 1))
+    upper = jnp.where(lane < HALO_CURVE, pltpu.roll(first, HALO_CURVE, 1), rest)
+    even = jnp.full(first.shape, lax.rem(lax.axis_index("dom"), 2), jnp.int32) == 0
+    near[...] = jnp.where(even, upper, lower)
+    far[...] = jnp.where(even, lower, upper)
     turned[...] = jnp.zeros_like(turned)
     wide = jnp.concatenate([chosen[:, LANES:], jnp.zeros((n.rows_pad - n.rows, n.slot_cols - LANES), F32)], axis=0)
     turned[...] = wide.T
-    here = lax.axis_index("sub")
     for k, ref in enumerate(peers):
-        block = lax.rem(here + k, n.subs)
+        block = peer_block(n, k, False)
         ref[...] = turned[pl.ds(pl.multiple_of(block * HALO_PEER, HALO_PEER), HALO_PEER), :]
 
 
-def first_kernel(n, dof, project, stiffness, star, send_element, send_face,
-                 first, second, table, lower, upper, *rest):
-    peers = rest[: n.subs]
-    left, onehot, right, spread, pad, keys, turned = rest[n.subs :]
+def first_kernel(n, *refs):
+    brought = refs[:FAR]
+    first, second, table, near, far = refs[FAR : FAR + 5]
+    peers = refs[FAR + 5 : FAR + 5 + n.subs]
+    left, onehot = refs[FAR + 5 + n.subs : FAR + 7 + n.subs]
+    kept = refs[FAR + 7 + n.subs : 2 * FAR + 5 + n.subs]
+    right, spread, pad, keys, turned, send_element, send_face, arrived = refs[2 * FAR + 5 + n.subs :]
+    copies = [pltpu.make_async_copy(src, dst, arrived.at[i])
+              for i, (src, dst) in enumerate(zip(brought, (send_element, send_face) + tuple(kept)))]
+    for c in copies:
+        c.start()
+    project, stiffness, dof, star = kept[:4]
+    for c in copies[:5]:
+        c.wait()
+    send_onehot(n, onehot, keys, send_element, send_face)
     fill_left(n, left, None, pad, project, [stiffness[d].T for d in range(3)])
-    send_onehot(n, onehot, keys, send_element, send_face)
     for v in range(n.nvar):
         x = dof[v]
         first[:, n.var(v)] = x
         second[:, n.var(v)] = x
     fill_right(n, right, first)
+    copies[5].wait()
     predict(n, left, right, spread, star, [first, second],
             lambda inv, two: [inv, (two - 1.0) * inv])
     fill_right(n, right, first)
-    traces_and_sends(n, left, right, table, onehot, turned, lower, upper, peers)
+    traces_and_sends(n, left, right, table, onehot, turned, near, far, peers)
+    for c in copies[6:]:
+        c.wait()
 
 
 def own_part(n, left, right, spread, star, flux_local, lift, solved, stacked, part):
@@ -266,17 +282,18 @@
     found[...] = dot(hi, onehot_own[...]) + dot(lo, onehot_own[...])
 
 
-def neighbour_part(n, below, above, peers, found, onehot_halo, flux_neighbour, masks, lift_turned,
+def neighbour_part(n, near, far, peers, found, onehot_halo, flux_neighbour, masks, lift_turned,
                    traces, solved, stacked, turned):
-    lane = lax.broadcasted_iota(jnp.int32, below.shape, 1)
-    b, a = below[...], above[...]
+    lane = lax.broadcasted_iota(jnp.int32, near.shape, 1)
+    even = jnp.full(near.shape, lax.rem(lax.axis_index("dom"), 2), jnp.int32) == 0
+    b = jnp.where(even, far[...], near[...])
+    a = jnp.where(even, near[...], far[...])
     first = jnp.where(lane < HALO_CURVE, b, pltpu.roll(a, HALO_CURVE, 1))
     rest = jnp.where(lane < HALO_CURVE, pltpu.roll(b, HALO_CURVE, 1), a)
     curve = jnp.concatenate([first, rest], axis=0)[: n.rows]
     turned[...] = jnp.zeros_like(turned)
-    here = lax.axis_index("sub")
     for k, ref in enumerate(peers):
-        block = lax.rem(here + n.subs - k, n.subs)
+        block = peer_block(n, k, True)
         turned[pl.ds(pl.multiple_of(block * HALO_PEER, HALO_PEER), HALO_PEER), :] = ref[...]
     flat = turned[...].T[: n.rows, :]
     hi, lo = halves(jnp.concatenate([curve, flat], axis=1))
@@ -302,13 +319,13 @@
 
 
 def third_kernel(n, *refs):
-    below, above = refs[:2]
+    near, far = refs[:2]
     peers = refs[2 : 2 + n.subs]
     (found, onehot_halo, flux_neighbour, masks, lift_turned, part, dof, labels, second, star, left, send_onehot_ref,
-     later, middle, traces, table, lower, upper) = refs[2 + n.subs : 20 + n.subs]
+     later, middle, traces, table, near_out, far_out) = refs[2 + n.subs : 20 + n.subs]
     sent = refs[20 + n.subs : 20 + 2 * n.subs]
     right, spread, solved, stacked, turned = refs[20 + 2 * n.subs :]
-    neighbour_part(n, below, above, peers, found, onehot_halo, flux_neighbour, masks, lift_turned,
+    neighbour_part(n, near, far, peers, found, onehot_halo, flux_neighbour, masks, lift_turned,
                    traces, solved, stacked, turned)
     fine = labels[...] == 0
     for c0, cn in n.chunks:
@@ -327,7 +344,7 @@
         c = n.var(v)
         later[:, c] = jnp.where(fine, later[:, c], second[:, c])
     fill_right(n, right, later)
-    traces_and_sends(n, left, right, table, send_onehot_ref, turned, lower, upper, sent)
+    traces_and_sends(n, left, right, table, send_onehot_ref, turned, near_out, far_out, sent)
 
 
 def fourth_kernel(n, first, second, later, middle, labels, star, left, flux_local, lift, table, onehot_own, traces,
@@ -348,44 +365,63 @@
 
 
 def fifth_kernel(n, *refs):
-    below, above = refs[:2]
+    near, far = refs[:2]
     peers = refs[2 : 2 + n.subs]
-    found, onehot_halo, flux_neighbour, masks, lift_turned, part, out, traces, solved, stacked, turned = refs[2 + n.subs :]
-    neighbour_part(n, below, above, peers, found, onehot_halo, flux_neighbour, masks, lift_turned,
+    (found, onehot_halo, flux_neighbour, masks, lift_turned, part, out,
+     traces, solved, stacked, turned, result, left_for) = refs[2 + n.subs :]
+    neighbour_part(n, near, far, peers, found, onehot_halo, flux_neighbour, masks, lift_turned,
                    traces, solved, stacked, turned)
+    copies = []
     for c0, cn in n.chunks:
         got = dot(lift_turned[...], stacked[:, c0 : c0 + cn])
         nb = got[: n.basis] + got[n.basis :]
         for v in range(c0 // n.elements, (c0 + cn) // n.elements):
             o = v * n.elements - c0
-            out[v] = part[:, n.var(v)] - nb[:, o : o + n.elements]
-
-
-def call(kernel, n, operands, outs, scratch, name):
-    vm = pl.BlockSpec(memory_space=pltpu.VMEM)
+            result[v] = part[:, n.var(v)] - nb[:, o : o + n.elements]
+            copies.append(pltpu.make_async_copy(result.at[v], out.at[v], left_for.at[v]))
+            copies[-1].start()
+    for c in copies:
+        c.wait()
+
+
+def call(kernel, n, operands, outs, scratch, name, far_in=False, far_out=False):
+    near, far = pltpu.VMEM, pltpu.HBM
+    place = far if far_in else near
 
     def body(*refs):
         kernel(n, *refs)
 
     return pl.pallas_call(
         body,
-        out_shape=[jax.ShapeDtypeStruct(s, t) for s, t in outs],
-        in_specs=[vm] * len(operands),
-        out_specs=[vm] * len(outs),
-        scratch_shapes=[pltpu.VMEM(s, t) for s, t in scratch],
+        out_shape=[(far if far_out else near)(s, t) for s, t in outs],
+        in_specs=[pl.BlockSpec(memory_space=place)] * len(operands),
+        out_specs=[pl.BlockSpec(memory_space=far if far_out else near)] * len(outs),
+        scratch_shapes=scratch,
+        compiler_params=pltpu.CompilerParams(vmem_limit_bytes=24 << 20),
         name=name,
-    )(*operands)
-
-
-def ring(value, axis, by):
-    peers = lax.axis_size(axis)
-    return lax.ppermute(value, axis, [(i, (i + by) % peers) for i in range(peers)])
-
-
-def exchange(lower, upper, peers):
-    below = ring(upper, "dom", 1)
-    above = ring(lower, "dom", -1)
-    return [below, above, peers[0]] + [ring(p, "sub", k) for k, p in enumerate(peers) if k]
+    )(*[pltpu.with_memory_space_constraint(x, place) for x in operands])
+
+
+def along(value, axis, partner):
+    count = lax.axis_size(axis)
+    pairs = [(i, partner(i)) for i in range(count)]
+    return lax.ppermute(value, axis, [(i, j if 0 <= j < count else i) for i, j in pairs])
+
+
+def exchange(near, far, peers):
+    count = lax.axis_size("sub")
+    swaps = count & (count - 1) == 0
+    got = [along(p, "sub", lambda i, k=k: i ^ k if swaps else (i + k) % count) for k, p in enumerate(peers) if k]
+    far = along(far, "dom", lambda i: i + 1 if i % 2 else i - 1)
+    near = along(near, "dom", lambda i: i ^ 1)
+    return [near, far, peers[0]] + got
+
+
+def peer_block(n, k, back):
+    here = lax.axis_index("sub")
+    if n.subs & (n.subs - 1) == 0:
+        return here ^ k
+    return lax.rem(here + (n.subs - k if back else k), n.subs)
 
 
 def per_device(dof_values, stiffness, face_project, face_lift, face_rotate, star_matrices, flux_local, flux_neighbour,
@@ -405,44 +441,54 @@
     pack = ((n.half, LANES), F32)
     peer = ((HALO_PEER, n.rows_pad), F32)
     left_t = ((n.left_rows, 3 * KB), BF16)
-    right_t = ((3 * KB, n.width), BF16)
-    spread_t = ((n.left_rows, n.width), F32)
-    turned_t = ((n.slot_cols - LANES, n.rows_pad), F32)
-    solved_t = ((n.fm, n.width), F32)
-    own_stack = ((2 * LANES, n.width), BF16)
     rot_rows = up(3 * n.fm, LANES)
-    rot_stack = ((2 * rot_rows, n.width), BF16)
-    pad_t = ((n.left_rows, LANES), F32)
-
+    right_t = pltpu.VMEM((3 * KB, n.width), BF16)
+    spread_t = pltpu.VMEM((n.left_rows, n.width), F32)
+    turned_t = pltpu.VMEM((n.slot_cols - LANES, n.rows_pad), F32)
+    solved_t = pltpu.VMEM((n.fm, n.width), F32)
+    own_stack = pltpu.VMEM((2 * LANES, n.width), BF16)
+    rot_stack = pltpu.VMEM((2 * rot_rows, n.width), BF16)
+    pad_t = pltpu.VMEM((n.left_rows, LANES), F32)
+
+    sends = [send_element, send_face]
+    kept = [project, stiffness, dof, star, lift, face_rotate, local, remote, labels,
+            neighbour_index, neighbour_face, neighbour_orient]
     outs = call(
-        first_kernel, n, [dof, project, stiffness, star, send_element, send_face],
-        [field, field, grid, pack, pack] + [peer] * n.subs + [left_t, ((n.cols4, n.slot_cols), BF16)],
-        [right_t, spread_t, pad_t, ((8, n.slot_cols), jnp.int32), turned_t], "predict_first")
-    first, second, table, lower, upper = outs[:5]
+        first_kernel, n, sends + kept,
+        [field, field, grid, pack, pack] + [peer] * n.subs + [left_t, ((n.cols4, n.slot_cols), BF16)]
+        + [(x.shape, x.dtype) for x in kept],
+        [right_t, spread_t, pad_t, pltpu.VMEM((8, n.slot_cols), jnp.int32), turned_t]
+        + [pltpu.VMEM(x.shape, x.dtype) for x in sends] + [pltpu.SemaphoreType.DMA((FAR,))],
+        "predict_first", far_in=True)
+    first, second, table, near, far = outs[:5]
     peers = outs[5 : 5 + n.subs]
-    left_one, send_sel = outs[5 + n.subs :]
-    got = exchange(lower, upper, peers)
+    left_one, send_sel = outs[5 + n.subs : 7 + n.subs]
+    project, stiffness, dof, star, lift, face_rotate, local, remote, labels, index, face, orient = outs[7 + n.subs :]
+    got = exchange(near, far, peers)
     part, found, left_two, lift_own, lift_rot, sel_own, sel_halo, masks = call(
         second_kernel, n,
-        [first, table, project, stiffness, star, lift, face_rotate, local, neighbour_index, neighbour_face, neighbour_orient],
+        [first, table, project, stiffness, star, lift, face_rotate, local, index, face, orient],
         [field, grid, left_t, ((2 * n.basis, 2 * LANES), BF16), ((2 * n.basis, 2 * rot_rows), BF16),
          ((n.cols4, n.cols4), BF16), ((n.slot_cols, n.cols4), BF16), ((3 * n.fm, n.elements), BF16)],
-        [right_t, spread_t, pad_t, solved_t, own_stack, ((rot_rows, LANES), F32), ((2 * n.basis, rot_rows), F32),
-         ((LANES, LANES), F32), ((3 * n.fm, n.elements), F32)], "own_first")
+        [right_t, spread_t, pad_t, solved_t, own_stack]
+        + [pltpu.VMEM(s, F32) for s in ((rot_rows, LANES), (2 * n.basis, rot_rows), (LANES, LANES), (3 * n.fm, n.elements))],
+        "own_first")
     outs = call(
         third_kernel, n,
         got + [found, sel_halo, remote, masks, lift_rot, part, dof, labels, second, star, left_one, send_sel],
         [field, field, grid, grid, pack, pack] + [peer] * n.subs,
         [right_t, spread_t, solved_t, rot_stack, turned_t], "neighbour_first")
-    later, middle, traces, table, lower, upper = outs[:6]
-    got = exchange(lower, upper, outs[6:])
+    later, middle, traces, table, near, far = outs[:6]
+    got = exchange(near, far, outs[6:])
     part, found = call(
         fourth_kernel, n,
         [first, second, later, middle, labels, star, left_two, local, lift_own, table, sel_own, traces],
         [field, grid], [right_t, spread_t, solved_t, own_stack], "own_second")
     (out,) = call(
         fifth_kernel, n, got + [found, sel_halo, remote, masks, lift_rot, part],
-        [((n.nvar, n.basis, n.elements), F32)], [grid, solved_t, rot_stack, turned_t], "neighbour_second")
+        [((n.nvar, n.basis, n.elements), F32)],
+        [pltpu.VMEM(*grid), solved_t, rot_stack, turned_t, pltpu.VMEM((n.nvar, n.basis, n.elements), F32),
+         pltpu.SemaphoreType.DMA((n.nvar,))], "neighbour_second", far_out=True)
     return jnp.transpose(out, (1, 0, 2))
 
 

time: 45.4 us -> 37.6 us (0.83)
  the two profiles are of different devices: /device:TPU:0 before, /device:TPU:6 now
where the time goes in v1:
time: 37.6 us; the launch traced here: 37.4 us
  Pallas kernels  18.7 us (50%)
  starting transfers between devices  15 us (40%)
  waiting for transfers between devices  3.57 us (9%)
    pallas_call x5, Pallas kernels, call(): pl.pallas_call(body, out_shape=[(far if far_out else near)(s, t) for s, t...  18.7 us
    ppermute x10, starting transfers between devices, along(): lax.ppermute(value, axis, [(i, j if 0 <= j < count else i) for i, j in pa...  15 us
    ppermute x10, waiting for transfers between devices, along(): lax.ppermute(value, axis, [(i, j if 0 <= j < count else i) for i, j in pa...  3.57 us
  transfers between devices with their start and end apart: 10, of which 2 were waited for; matrix products, arithmetic and copies ran while one was open for 0% of the time, Pallas kernels for 10%

profile of v1, /device:TPU:6, one launch (start us, length us, event | category | flops | bytes accessed | tf_op | source)
XLA Modules:
  0.0 37.4 jit_solution(18283459112520600964)
XLA Ops:
  0.0 6.6 %predict_first.1 = (f32[56,1152]{1,0:T(8,128)S(1)}, f32[56,1152]{1,0:T(8,128)S(1)}, f32[216,512]{1,0:T(8,128)S(1)}, f32[112,128]{1,0:T(8,128)S(1)}, f32[112,128]...) custom-call(s32[1,160]{1,0:T(1,128)} %refs_0_.1, ...), custom_call_target="tpu_custom_call" | custom-call | tf_op jit(solution)/shard_map/predict_first/pallas_call | solution.py:394
  6.7 0.1 collective-permute-start
  6.7 2.5 %collective-permute-start.1 = (f32[112,128]{1,0:T(8,128)S(1)}, f32[112,128]{1,0:T(8,128)S(1)}, u32[]{:S(2)}, u32[]{:S(2)}) collective-permute-start(f32[112,128]{1,0:T(8,128)S(1)} %get-tuple-element.49), channel_id=1, source_target_pairs={{0,0},{4,8},{8,4},{12,16},{16,12},{20,24},{24,20},{28,28},{1,1},{5... | collective-permute-start | bytes 172040 | tf_op jit(solution)/shard_map/ppermute | solution.py:408
  9.3 1.6 %collective-permute-start.2 = (f32[8,256]{1,0:T(8,128)S(1)}, f32[8,256]{1,0:T(8,128)S(1)}, u32[]{:S(2)}, u32[]{:S(2)}) collective-permute-start(f32[8,256]{1,0:T(8,128)S(1)} %get-tuple-element.51), channel_id=1, source_target_pairs={{0,1},{1,0},{2,3},{3,2},{4,5},{5,4},{6,7},{7,6},{8,9},{9,8},{10,11... | collective-permute-start | bytes 24584 | tf_op jit(solution)/shard_map/ppermute | solution.py:408
  10.9 2.6 %collective-permute-start.3 = (f32[8,256]{1,0:T(8,128)S(1)}, f32[8,256]{1,0:T(8,128)S(1)}, u32[]{:S(2)}, u32[]{:S(2)}) collective-permute-start(f32[8,256]{1,0:T(8,128)S(1)} %get-tuple-element.52), channel_id=1, source_target_pairs={{0,2},{1,3},{2,0},{3,1},{4,6},{5,7},{6,4},{7,5},{8,10},{9,11},{10,... | collective-permute-start | bytes 24584 | tf_op jit(solution)/shard_map/ppermute | solution.py:408
  13.5 0.2 collective-permute-start.4
  13.7 2.2 %own_first.1 = (f32[56,1152]{1,0:T(8,128)S(1)}, f32[216,512]{1,0:T(8,128)S(1)}, bf16[264,192]{1,0:T(8,128)(2,1)S(1)}, bf16[112,256]{1,0:T(8,128)(2,1)S(1)}, bf16...) custom-call(f32[56,1152]{1,0:T(8,128)S(1)} %get-tuple-element.54.ref, ...), custom_call_target="tpu_custom_call" | custom-call | tf_op jit(solution)/shard_map/own_first/pallas_call | solution.py:394
  15.9 0.0 collective-permute-done.2.refs_3_
  15.9 0.0 collective-permute-done.3.refs_4_
  15.9 3.0 %collective-permute-done.4.refs_5_ = f32[8,256]{1,0:T(8,128)S(1)} collective-permute-done((f32[8,256]{1,0:T(8,128)S(1)}, f32[8,256]{1,0:T(8,128)S(1)}, u32[]{:S(2)}, u32[]{:S(2)}) %collective-permute-start.4) | collective-permute-done | bytes 8224 | tf_op jit(solution)/shard_map/ppermute | solution.py:408
  19.0 0.0 collective-permute-done.refs_0_
  19.0 0.0 collective-permute-done.1.refs_1_
  19.0 6.3 %neighbour_first.1 = (f32[56,1152]{1,0:T(8,128)S(1)}, f32[56,1152]{1,0:T(8,128)S(1)}, f32[216,512]{1,0:T(8,128)S(1)}, f32[216,512]{1,0:T(8,128)S(1)}, f32[112,12...) custom-call(f32[112,128]{1,0:T(8,128)S(1)} %collective-permute-done., ...), custom_call_target="tpu_custom_call" | custom-call | tf_op jit(solution)/shard_map/neighbour_first/pallas_call | solution.py:394
  25.3 0.1 collective-permute-start.5
  25.3 3.4 %collective-permute-start.6 = (f32[112,128]{1,0:T(8,128)S(1)}, f32[112,128]{1,0:T(8,128)S(1)}, u32[]{:S(2)}, u32[]{:S(2)}) collective-permute-start(f32[112,128]{1,0:T(8,128)S(1)} %get-tuple-element.77), channel_id=1, source_target_pairs={{0,0},{4,8},{8,4},{12,16},{16,12},{20,24},{24,20},{28,28},{1,1},{5... | collective-permute-start | bytes 172040 | tf_op jit(solution)/shard_map/ppermute | solution.py:408
  28.8 0.1 collective-permute-start.7
  28.9 1.1 %collective-permute-start.8 = (f32[8,256]{1,0:T(8,128)S(1)}, f32[8,256]{1,0:T(8,128)S(1)}, u32[]{:S(2)}, u32[]{:S(2)}) collective-permute-start(f32[8,256]{1,0:T(8,128)S(1)} %get-tuple-element.80), channel_id=1, source_target_pairs={{0,2},{1,3},{2,0},{3,1},{4,6},{5,7},{6,4},{7,5},{8,10},{9,11},{10,... | collective-permute-start | bytes 24584 | tf_op jit(solution)/shard_map/ppermute | solution.py:408
  30.0 3.2 %collective-permute-start.9 = (f32[8,256]{1,0:T(8,128)S(1)}, f32[8,256]{1,0:T(8,128)S(1)}, u32[]{:S(2)}, u32[]{:S(2)}) collective-permute-start(f32[8,256]{1,0:T(8,128)S(1)} %get-tuple-element.81), channel_id=1, source_target_pairs={{0,3},{1,2},{2,1},{3,0},{4,7},{5,6},{6,5},{7,4},{8,11},{9,10},{10,... | collective-permute-start | bytes 24584 | tf_op jit(solution)/shard_map/ppermute | solution.py:408
  33.2 1.7 %own_second.1 = (f32[56,1152]{1,0:T(8,128)S(1)}, f32[216,512]{1,0:T(8,128)S(1)}) custom-call(f32[56,1152]{1,0:T(8,128)S(1)} %get-tuple-element.54.refs_0_, f32[56,1152]{1,0:T(8,128)S(1)} %get-tuple-element.73.refs_14_.refs_1_, f32[56,1152]{1,0:T(8,128)S(1)} %get-tuple-element.82.refs_2_, f32[56,1152]{1,0:T(8,128)S(1)} %get-tuple-element.83.refs_3_, ...), custom_call_target="tpu_custom_call" | custom-call | tf_op jit(solution)/shard_map/own_second/pallas_call | solution.py:394
  34.9 0.0 collective-permute-done.7.refs_3_
  34.9 0.0 collective-permute-done.8.refs_4_
  34.9 0.5 %collective-permute-done.9.refs_5_ = f32[8,256]{1,0:T(8,128)S(1)} collective-permute-done((f32[8,256]{1,0:T(8,128)S(1)}, f32[8,256]{1,0:T(8,128)S(1)}, u32[]{:S(2)}, u32[]{:S(2)}) %collective-permute-start.9) | collective-permute-done | bytes 8224 | tf_op jit(solution)/shard_map/ppermute | solution.py:408
  35.5 0.0 collective-permute-done.5.refs_0_
  35.5 0.0 collective-permute-done.6.refs_1_
  35.5 1.9 %neighbour_second.1 = f32[9,56,128]{2,1,0:T(8,128)} custom-call(f32[112,128]{1,0:T(8,128)S(1)} %collective-permute-done.5.refs_0_, f32[112,128]{1,0:T(8,128)S(1)} %collective-permute-done.6.refs_1_, f32[8,256]{1,0:T(8,128)S(1)} %get-tuple-element.78.refs_2_, f32[8,256]{1,0:T(8,128)S(1)} %collective-permute-done.7.refs_3_, ...), custom_call_target="tpu_custom_call" | custom-call | tf_op jit(solution)/shard_map/neighbour_second/pallas_call | solution.py:394
Async XLA Ops:
  6.7 12.3 %collective-permute-start = (f32[112,128]{1,0:T(8,128)S(1)}, f32[112,128]{1,0:T(8,128)S(1)}, u32[]{:S(2)}, u32[]{:S(2)}) collective-permute-start(f32[112,128]{1,0:T(8,128)S(1)} %get-tuple-element.48), channel_id=1, source_target_pairs={{0,4},{4,0},{8,12},{12,8},{16,20},{20,16},{24,28},{28,24},{1,5},{5... | collective-permute-start | bytes 172040 | tf_op jit(solution)/shard_map/ppermute | solution.py:408
  6.7 12.2 %collective-permute-start.1 = (f32[112,128]{1,0:T(8,128)S(1)}, f32[112,128]{1,0:T(8,128)S(1)}, u32[]{:S(2)}, u32[]{:S(2)}) collective-permute-start(f32[112,128]{1,0:T(8,128)S(1)} %get-tuple-element.49), channel_id=1, source_target_pairs={{0,0},{4,8},{8,4},{12,16},{16,12},{20,24},{24,20},{28,28},{1,1},{5... | collective-permute-start | bytes 172040 | tf_op jit(solution)/shard_map/ppermute | solution.py:408
  9.3 6.6 %collective-permute-start.2 = (f32[8,256]{1,0:T(8,128)S(1)}, f32[8,256]{1,0:T(8,128)S(1)}, u32[]{:S(2)}, u32[]{:S(2)}) collective-permute-start(f32[8,256]{1,0:T(8,128)S(1)} %get-tuple-element.51), channel_id=1, source_target_pairs={{0,1},{1,0},{2,3},{3,2},{4,5},{5,4},{6,7},{7,6},{8,9},{9,8},{10,11... | collective-permute-start | bytes 24584 | tf_op jit(solution)/shard_map/ppermute | solution.py:408
  10.9 5.0 %collective-permute-start.3 = (f32[8,256]{1,0:T(8,128)S(1)}, f32[8,256]{1,0:T(8,128)S(1)}, u32[]{:S(2)}, u32[]{:S(2)}) collective-permute-start(f32[8,256]{1,0:T(8,128)S(1)} %get-tuple-element.52), channel_id=1, source_target_pairs={{0,2},{1,3},{2,0},{3,1},{4,6},{5,7},{6,4},{7,5},{8,10},{9,11},{10,... | collective-permute-start | bytes 24584 | tf_op jit(solution)/shard_map/ppermute | solution.py:408
  13.5 5.4 %collective-permute-start.4 = (f32[8,256]{1,0:T(8,128)S(1)}, f32[8,256]{1,0:T(8,128)S(1)}, u32[]{:S(2)}, u32[]{:S(2)}) collective-permute-start(f32[8,256]{1,0:T(8,128)S(1)} %get-tuple-element.53), channel_id=1, source_target_pairs={{0,3},{1,2},{2,1},{3,0},{4,7},{5,6},{6,5},{7,4},{8,11},{9,10},{10,... | collective-permute-start | bytes 24584 | tf_op jit(solution)/shard_map/ppermute | solution.py:408
  25.3 10.2 %collective-permute-start.5 = (f32[112,128]{1,0:T(8,128)S(1)}, f32[112,128]{1,0:T(8,128)S(1)}, u32[]{:S(2)}, u32[]{:S(2)}) collective-permute-start(f32[112,128]{1,0:T(8,128)S(1)} %get-tuple-element.76), channel_id=1, source_target_pairs={{0,4},{4,0},{8,12},{12,8},{16,20},{20,16},{24,28},{28,24},{1,5},{5... | collective-permute-start | bytes 172040 | tf_op jit(solution)/shard_map/ppermute | solution.py:408
  25.3 10.1 %collective-permute-start.6 = (f32[112,128]{1,0:T(8,128)S(1)}, f32[112,128]{1,0:T(8,128)S(1)}, u32[]{:S(2)}, u32[]{:S(2)}) collective-permute-start(f32[112,128]{1,0:T(8,128)S(1)} %get-tuple-element.77), channel_id=1, source_target_pairs={{0,0},{4,8},{8,4},{12,16},{16,12},{20,24},{24,20},{28,28},{1,1},{5... | collective-permute-start | bytes 172040 | tf_op jit(solution)/shard_map/ppermute | solution.py:408
  28.8 6.1 %collective-permute-start.7 = (f32[8,256]{1,0:T(8,128)S(1)}, f32[8,256]{1,0:T(8,128)S(1)}, u32[]{:S(2)}, u32[]{:S(2)}) collective-permute-start(f32[8,256]{1,0:T(8,128)S(1)} %get-tuple-element.79), channel_id=1, source_target_pairs={{0,1},{1,0},{2,3},{3,2},{4,5},{5,4},{6,7},{7,6},{8,9},{9,8},{10,11... | collective-permute-start | bytes 24584 | tf_op jit(solution)/shard_map/ppermute | solution.py:408
  28.9 6.1 %collective-permute-start.8 = (f32[8,256]{1,0:T(8,128)S(1)}, f32[8,256]{1,0:T(8,128)S(1)}, u32[]{:S(2)}, u32[]{:S(2)}) collective-permute-start(f32[8,256]{1,0:T(8,128)S(1)} %get-tuple-element.80), channel_id=1, source_target_pairs={{0,2},{1,3},{2,0},{3,1},{4,6},{5,7},{6,4},{7,5},{8,10},{9,11},{10,... | collective-permute-start | bytes 24584 | tf_op jit(solution)/shard_map/ppermute | solution.py:408
  30.0 5.4 %collective-permute-start.9 = (f32[8,256]{1,0:T(8,128)S(1)}, f32[8,256]{1,0:T(8,128)S(1)}, u32[]{:S(2)}, u32[]{:S(2)}) collective-permute-start(f32[8,256]{1,0:T(8,128)S(1)} %get-tuple-element.81), channel_id=1, source_target_pairs={{0,3},{1,2},{2,1},{3,0},{4,7},{5,6},{6,5},{7,4},{8,11},{9,10},{10,... | collective-permute-start | bytes 24584 | tf_op jit(solution)/shard_map/ppermute | solution.py:408

commit v2 on v1

v2 whole, which is shorter than its diff:
```python
import jax
import jax.numpy as jnp
from jax import lax
from jax.experimental import pallas as pl
from jax.experimental.pallas import tpu as pltpu
from jax.sharding import PartitionSpec as P


TAYLOR_TERMS = 6
HALO_CURVE = 64
HALO_PEER = 8
F32 = jnp.float32
BF16 = jnp.bfloat16
LANES = 128
FAR = 14
KB = 64


def up(n, m):
    return -(-n // m) * m


def halves(x):
    hi = x.astype(BF16)
    return hi, (x - hi.astype(F32)).astype(BF16)


def dot(a, b):
    return jnp.dot(a, b, preferred_element_type=F32)


class Dims:
    def __init__(self, basis, nvar, elements, fbasis, slots, subs):
        self.basis, self.nvar, self.elements, self.fbasis = basis, nvar, elements, fbasis
        self.slots, self.subs = slots, subs
        self.mp = up(fbasis, 8)
        self.fm = 4 * self.mp
        self.rows = nvar * self.mp
        self.width = nvar * elements
        self.cols4 = 4 * elements
        self.slot_cols = up(slots, LANES)
        self.half = up(-(-self.rows // 2), 8)
        self.rows_pad = up(self.rows, LANES)
        self.left_rows = self.fm + 3 * basis
        self.face_groups = [(r0, min(16, self.mp - r0)) for r0 in range(0, self.mp, 16)]
        self.chunks = []
        c0 = 0
        while c0 < self.width:
            cn = min(2 * elements, self.width - c0)
            self.chunks.append((c0, cn))
            c0 += cn

    def var(self, v):
        return slice(v * self.elements, (v + 1) * self.elements)


def fill_left(n, left, pad, project, mats):
    pad[...] = jnp.zeros_like(pad)
    for m in range(n.fbasis):
        for g in range(4):
            r = g * n.mp + m
            pad[r : r + 1, : n.basis] = project[m, g : g + 1, :]
    for d in range(3):
        r = n.fm + d * n.basis
        pad[r : r + n.basis, : n.basis] = mats[d]
    w = pad[...]
    hi = w.astype(BF16).astype(F32)
    lo = w - hi
    left[:, :LANES] = (hi + pltpu.roll(lo, KB, 1)).astype(BF16)
    left[:, LANES : LANES + KB] = hi[:, :KB].astype(BF16)


def put(n, right, r0, v, x):
    rows = x.shape[0]
    if rows % 16:
        x = jnp.concatenate([x, jnp.zeros((16 - rows % 16, x.shape[1]), F32)], axis=0)
        rows = x.shape[0]
    hi, lo = halves(x)
    c = n.var(v)
    right[r0 : r0 + rows, c] = hi
    right[KB + r0 : KB + r0 + rows, c] = hi
    right[2 * KB + r0 : 2 * KB + r0 + rows, c] = lo


def mix(n, load, terms, coef, outs=None):
    outs = range(n.nvar) if outs is None else outs
    acc = {}
    for v in range(n.nvar):
        for k in range(terms):
            t = load(v, k)
            for w in outs:
                p = t * coef(v, w, k)
                acc[w] = acc[w] + p if w in acc else p
    return acc


def spread_rows(n, spread, left, right, r, rows):
    for c0, cn in n.chunks:
        spread[r : r + rows, c0 : c0 + cn] = dot(left[r : r + rows, :], right[:, c0 : c0 + cn])


def block_of(n, c0, cn):
    return range(c0 // n.elements, (c0 + cn) // n.elements)


def star_mix(n, spread, star, outs):
    def load(v, d):
        r = n.fm + d * n.basis
        return spread[r : r + n.basis, n.var(v)]

    return mix(n, load, 3, lambda v, w, d: star[v, w, d : d + 1, :], outs)


def predict(n, left, right, spreads, star, sums, weights):
    def step(k, inv, two, now, later):
        inv = inv / (k + 1)
        two = two * 2.0
        scale = weights(inv, two)
        for c0, cn in n.chunks:
            for w, x in star_mix(n, now, star, block_of(n, c0, cn)).items():
                for field, s in zip(sums, scale):
                    field[:, n.var(w)] += s * x
                if later is not None:
                    put(n, right, 0, w, x)
            if later is not None:
                later[n.fm :, c0 : c0 + cn] = dot(left[n.fm :, :], right[:, c0 : c0 + cn])
        return inv, two

    def body(j, carry):
        k = (2 * j).astype(F32)
        carry = step(k + 1.0, *carry, spreads[0], spreads[1])
        return step(k + 2.0, *carry, spreads[1], spreads[0])

    spread_rows(n, spreads[0], left, right, n.fm, 3 * n.basis)
    steps = TAYLOR_TERMS - 1
    carry = lax.fori_loop(0, (steps - 1) // 2, body, (jnp.float32(1.0), jnp.float32(2.0)))
    step(float(steps), *carry, spreads[0], None)


def fill_right(n, right, field):
    for v in range(n.nvar):
        put(n, right, 0, v, field[:, n.var(v)])


def lane_pick(x, lanes):
    return jnp.take_along_axis(x, jnp.broadcast_to(lanes, x.shape), axis=1, mode="promise_in_bounds")


def face_pick(n, table, element, face):
    got = lane_pick(table[:, n.var(0)], element)
    for g in range(1, 4):
        got = jnp.where(face == g, lane_pick(table[:, n.var(g)], element), got)
    return got


def own_traces(n, table, index, face, f):
    idx = index[f : f + 1, :]
    return jnp.where(idx < n.elements, face_pick(n, table, idx & (n.elements - 1), face[f : f + 1, :]), 0.0)


def halo_slots(n, index, f):
    dom = lax.axis_index("dom")
    last = lax.axis_size("dom") - 1
    slot = index[f : f + 1, :] - n.elements
    slot = jnp.where(jnp.logical_and(slot < HALO_CURVE, dom == 0), -1, slot)
    high = jnp.logical_and(slot >= HALO_CURVE, slot < 2 * HALO_CURVE)
    return jnp.where(jnp.logical_and(high, dom == last), -1, slot)


def traces_and_sends(n, left, right, table, sends, turned, near, far, peers):
    for c0, cn in n.chunks:
        p = dot(left[: n.fm, :], right[:, c0 : c0 + cn])
        for v in range(c0 // n.elements, (c0 + cn) // n.elements):
            o = v * n.elements - c0
            for g in range(4):
                table[v * n.mp : (v + 1) * n.mp, n.var(g)] = p[g * n.mp : (g + 1) * n.mp, o : o + n.elements]
    chosen = [face_pick(n, table, sends[0:1, c : c + LANES], sends[1:2, c : c + LANES])
              for c in range(0, n.slot_cols, LANES)]
    curve = chosen[0]
    first, rest = curve[: n.half], curve[n.half :]
    short = n.half - rest.shape[0]
    if short:
        rest = jnp.concatenate([rest, jnp.zeros((short, LANES), F32)], axis=0)
    lane = lax.broadcasted_iota(jnp.int32, first.shape, 1)
    lower = jnp.where(lane < HALO_CURVE, first, pltpu.roll(rest, HALO_CURVE, 1))
    upper = jnp.where(lane < HALO_CURVE, pltpu.roll(first, HALO_CURVE, 1), rest)
    even = jnp.full(first.shape, lax.rem(lax.axis_index("dom"), 2), jnp.int32) == 0
    near[...] = jnp.where(even, upper, lower)
    far[...] = jnp.where(even, lower, upper)
    turned[...] = jnp.zeros_like(turned)
    wide = jnp.concatenate([jnp.concatenate(chosen[1:], axis=1), jnp.zeros((n.rows_pad - n.rows, n.slot_cols - LANES), F32)], axis=0)
    turned[...] = wide.T
    for k, ref in enumerate(peers):
        block = peer_block(n, k, False)
        ref[...] = turned[pl.ds(pl.multiple_of(block * HALO_PEER, HALO_PEER), HALO_PEER), :]


def first_kernel(n, *refs):
    brought = refs[:FAR]
    first, second, table, near, far = refs[FAR : FAR + 5]
    peers = refs[FAR + 5 : FAR + 5 + n.subs]
    left, sends = refs[FAR + 5 + n.subs : FAR + 7 + n.subs]
    kept = refs[FAR + 7 + n.subs : 2 * FAR + 5 + n.subs]
    right, spread, held, pad, turned, send_element, send_face, arrived = refs[2 * FAR + 5 + n.subs :]
    copies = [pltpu.make_async_copy(src, dst, arrived.at[i])
              for i, (src, dst) in enumerate(zip(brought, (send_element, send_face) + tuple(kept)))]
    for c in copies[2:6] + copies[:2]:
        c.start()
    project, stiffness, dof, star = kept[:4]
    for c in copies[2:4]:
        c.wait()
    fill_left(n, left, pad, project, [stiffness[d].T for d in range(3)])
    copies[4].wait()
    for v in range(n.nvar):
        x = dof[v]
        first[:, n.var(v)] = x
        second[:, n.var(v)] = x
    fill_right(n, right, first)
    for c in copies[:2]:
        c.wait()
    sends[...] = jnp.zeros_like(sends)
    sends[0:1, : n.slots] = send_element[...]
    sends[1:2, : n.slots] = send_face[...]
    copies[5].wait()
    for c in copies[6:]:
        c.start()
    predict(n, left, right, [spread, held], star, [first, second],
            lambda inv, two: [inv, (two - 1.0) * inv])
    fill_right(n, right, first)
    traces_and_sends(n, left, right, table, sends, turned, near, far, peers)
    for c in copies[6:]:
        c.wait()


def own_part(n, left, right, spread, star, flux_local, lift, solved, stacked, part):
    spread_rows(n, spread, left, right, 0, n.fm)
    for g in range(4):
        for r0, rn in n.face_groups:
            r = g * n.mp + r0

            def load(v, k, r=r, rn=rn):
                return spread[r : r + rn, n.var(v)]

            acc = mix(n, load, 1, lambda v, w, k, g=g: flux_local[v, w, g : g + 1, :])
            for w in range(n.nvar):
                solved[r : r + rn, n.var(w)] = acc[w]
    for w in range(n.nvar):
        hi, lo = halves(solved[:, n.var(w)])
        stacked[: n.fm, n.var(w)] = hi
        stacked[LANES : LANES + n.fm, n.var(w)] = lo
    stacked[n.fm : LANES, :] = jnp.zeros((LANES - n.fm, n.width), BF16)
    stacked[LANES + n.fm :, :] = jnp.zeros((LANES - n.fm, n.width), BF16)
    spread_rows(n, spread, left, right, n.fm, 3 * n.basis)
    for c0, cn in n.chunks:
        for w, x in star_mix(n, spread, star, block_of(n, c0, cn)).items():
            part[:, n.var(w)] = x
    for c0, cn in n.chunks:
        out = dot(lift[...], stacked[:, c0 : c0 + cn])
        part[:, c0 : c0 + cn] = part[:, c0 : c0 + cn] - (out[: n.basis] + out[n.basis :])


def lift_rows(n, out, tall, w):
    hi = w.astype(BF16).astype(F32)
    lo = w - hi
    span = w.shape[1]
    tall[: n.basis, :span] = hi
    tall[n.basis : 2 * n.basis, :span] = lo
    out[:, :span] = tall[: 2 * n.basis, :span].astype(BF16)
    tall[n.basis : 2 * n.basis, :span] = jnp.zeros_like(lo)
    out[:, span:] = tall[: 2 * n.basis, :span].astype(BF16)


def second_kernel(n, field, table, project, stiffness, star, face_lift, face_rotate, flux_local, index, face, orient,
                  part, found, left, lift, lift_turned, masks,
                  right, spread, pad, solved, stacked, wide, tall, square, mask_rows):
    fill_left(n, left, pad, project, [stiffness[d] for d in range(3)])
    fill_right(n, right, field)
    wide[...] = jnp.zeros_like(wide)
    square[...] = jnp.zeros_like(square)
    for m in range(n.fbasis):
        for g in range(4):
            r = g * n.mp + m
            square[r : r + 1, : n.basis] = face_lift[m, g : g + 1, :]
    base = square[...]
    lift_rows(n, lift, tall, base.T[: n.basis, :])
    for o in range(3):
        square[...] = jnp.zeros_like(square)
        square[: n.fbasis, : n.fbasis] = face_rotate[o]
        turn = square[...].T[: n.mp, :]
        turn = turn[:, : n.mp]
        for g in range(4):
            r = o * n.fm + g * n.mp
            wide[r : r + n.mp, :] = jnp.dot(turn, base[g * n.mp : (g + 1) * n.mp, :],
                                            precision=lax.Precision.HIGHEST, preferred_element_type=F32)
    blocks = wide.shape[0] // LANES
    turned = jnp.concatenate([wide[i * LANES : (i + 1) * LANES, :].T[: n.basis, :] for i in range(blocks)], axis=1)
    lift_rows(n, lift_turned, tall, turned)
    for f in range(4):
        for o in range(3):
            r = o * n.fm + f * n.mp
            mask_rows[r : r + n.mp, :] = jnp.broadcast_to(
                jnp.where(orient[f : f + 1, :] == o, 1.0, 0.0), (n.mp, n.elements))
    masks[...] = mask_rows[...].astype(BF16)
    own_part(n, left, right, spread, star, flux_local, lift, solved, stacked, part)
    for f in range(4):
        found[:, n.var(f)] = own_traces(n, table, index, face, f)


def neighbour_part(n, near, far, peers, found, index, flux_neighbour, masks,
                   traces, solved, stacked, turned):
    lane = lax.broadcasted_iota(jnp.int32, near.shape, 1)
    even = jnp.full(near.shape, lax.rem(lax.axis_index("dom"), 2), jnp.int32) == 0
    b = jnp.where(even, far[...], near[...])
    a = jnp.where(even, near[...], far[...])
    first = jnp.where(lane < HALO_CURVE, b, pltpu.roll(a, HALO_CURVE, 1))
    rest = jnp.where(lane < HALO_CURVE, pltpu.roll(b, HALO_CURVE, 1), a)
    curve = jnp.concatenate([first, rest], axis=0)[: n.rows]
    turned[...] = jnp.zeros_like(turned)
    for k, ref in enumerate(peers):
        block = peer_block(n, k, True)
        turned[pl.ds(pl.multiple_of(block * HALO_PEER, HALO_PEER), HALO_PEER), :] = ref[...]
    flat = turned[...].T[: n.rows, :]
    tiles = [curve] + [flat[:, c : c + LANES] for c in range(0, n.slot_cols - LANES, LANES)]
    for f in range(4):
        slot = halo_slots(n, index, f)
        got = 0.0
        for i, tile in enumerate(tiles):
            named = jnp.logical_and(slot >= i * LANES, slot < (i + 1) * LANES)
            got = jnp.where(named, lane_pick(tile, slot & (LANES - 1)), got)
        traces[:, n.var(f)] = found[:, n.var(f)] + got
        for r0, rn in n.face_groups:
            def load(v, k, f=f, r0=r0, rn=rn):
                return traces[v * n.mp + r0 : v * n.mp + r0 + rn, n.var(f)]

            acc = mix(n, load, 1, lambda v, w, k, f=f: flux_neighbour[v, w, f : f + 1, :])
            for w in range(n.nvar):
                solved[f * n.mp + r0 : f * n.mp + r0 + rn, n.var(w)] = acc[w]
    span = stacked.shape[0] // 2
    for w in range(n.nvar):
        hi, lo = halves(solved[:, n.var(w)])
        for o in range(3):
            m = masks[o * n.fm : (o + 1) * n.fm, :]
            stacked[o * n.fm : (o + 1) * n.fm, n.var(w)] = hi * m
            stacked[span + o * n.fm : span + (o + 1) * n.fm, n.var(w)] = lo * m
    gap = span - 3 * n.fm
    if gap:
        stacked[3 * n.fm : span, :] = jnp.zeros((gap, n.width), BF16)
        stacked[span + 3 * n.fm :, :] = jnp.zeros((gap, n.width), BF16)


def third_kernel(n, *refs):
    near, far = refs[:2]
    peers = refs[2 : 2 + n.subs]
    (found, index, flux_neighbour, masks, lift_turned, part, dof, labels, second, star, left, sends,
     later, middle, traces, table, near_out, far_out) = refs[2 + n.subs : 20 + n.subs]
    sent = refs[20 + n.subs : 20 + 2 * n.subs]
    right, spread, held, solved, stacked, turned = refs[20 + 2 * n.subs :]
    neighbour_part(n, near, far, peers, found, index, flux_neighbour, masks,
                   traces, solved, stacked, turned)
    fine = labels[...] == 0
    for c0, cn in n.chunks:
        out = dot(lift_turned[...], stacked[:, c0 : c0 + cn])
        nb = out[: n.basis] + out[n.basis :]
        for v in range(c0 // n.elements, (c0 + cn) // n.elements):
            c = n.var(v)
            o = v * n.elements - c0
            x = dof[v]
            mid = jnp.where(fine, x + (part[:, c] - nb[:, o : o + n.elements]), x)
            middle[:, c] = mid
            later[:, c] = mid
    fill_right(n, right, middle)
    predict(n, left, right, [spread, held], star, [later], lambda inv, two: [inv])
    for v in range(n.nvar):
        c = n.var(v)
        later[:, c] = jnp.where(fine, later[:, c], second[:, c])
    fill_right(n, right, later)
    traces_and_sends(n, left, right, table, sends, turned, near_out, far_out, sent)


def fourth_kernel(n, first, second, later, middle, labels, star, left, flux_local, lift, table, index, face, traces,
                  part, found, right, spread, solved, stacked):
    fine = labels[...] == 0
    for v in range(n.nvar):
        c = n.var(v)
        put(n, right, 0, v, jnp.where(fine, later[:, c], first[:, c] + second[:, c]))
    own_part(n, left, right, spread, star, flux_local, lift, solved, stacked, part)
    part[...] = middle[...] + part[...]
    for f in range(4):
        c = n.var(f)
        found[:, c] = own_traces(n, table, index, face, f) + jnp.where(fine, 0.0, traces[:, c])


def fifth_kernel(n, *refs):
    near, far = refs[:2]
    peers = refs[2 : 2 + n.subs]
    (found, index, flux_neighbour, masks, lift_turned, part, out,
     traces, solved, stacked, turned, result, left_for) = refs[2 + n.subs :]
    neighbour_part(n, near, far, peers, found, index, flux_neighbour, masks,
                   traces, solved, stacked, turned)
    copies = []
    for c0, cn in n.chunks:
        got = dot(lift_turned[...], stacked[:, c0 : c0 + cn])
        nb = got[: n.basis] + got[n.basis :]
        for v in range(c0 // n.elements, (c0 + cn) // n.elements):
            o = v * n.elements - c0
            result[v] = part[:, n.var(v)] - nb[:, o : o + n.elements]
            copies.append(pltpu.make_async_copy(result.at[v], out.at[v], left_for.at[v]))
            copies[-1].start()
    for c in copies:
        c.wait()


def call(kernel, n, operands, outs, scratch, far_in=False, far_out=False):
    near, far = pltpu.VMEM, pltpu.HBM
    place = far if far_in else near

    def body(*refs):
        kernel(n, *refs)

    return pl.pallas_call(
        body,
        out_shape=[(far if far_out else near)(s, t) for s, t in outs],
        in_specs=[pl.BlockSpec(memory_space=place)] * len(operands),
        out_specs=[pl.BlockSpec(memory_space=far if far_out else near)] * len(outs),
        scratch_shapes=scratch,
        compiler_params=pltpu.CompilerParams(vmem_limit_bytes=24 << 20),
    )(*[pltpu.with_memory_space_constraint(x, place) for x in operands])


def along(value, axis, partner):
    count = lax.axis_size(axis)
    pairs = [(i, partner(i)) for i in range(count)]
    return lax.ppermute(value, axis, [(i, j if 0 <= j < count else i) for i, j in pairs])


def exchange(near, far, peers):
    count = lax.axis_size("sub")
    swaps = count & (count - 1) == 0
    got = [peers[0]]
    far = along(far, "dom", lambda i: i + 1 if i % 2 else i - 1)
    for k, p in enumerate(peers):
        if k:
            got.append(along(p, "sub", lambda i, k=k: i ^ k if swaps else (i + k) % count))
    near = along(near, "dom", lambda i: i ^ 1)
    return [near, far] + got


def peer_block(n, k, back):
    here = lax.axis_index("sub")
    if n.subs & (n.subs - 1) == 0:
        return here ^ k
    return lax.rem(here + (n.subs - k if back else k), n.subs)


def per_device(dof_values, stiffness, face_project, face_lift, face_rotate, star_matrices, flux_local, flux_neighbour,
               cluster_labels, neighbour_index, neighbour_face, neighbour_orient, send_element, send_face):
    n = Dims(dof_values.shape[0], dof_values.shape[1], dof_values.shape[2], face_project.shape[1],
             send_element.shape[1], lax.axis_size("sub"))
    dof = jnp.transpose(dof_values, (1, 0, 2))
    star = jnp.transpose(star_matrices, (1, 2, 0, 3))
    local = jnp.transpose(flux_local, (1, 2, 0, 3))
    remote = jnp.transpose(flux_neighbour, (1, 2, 0, 3))
    project = jnp.transpose(face_project, (1, 0, 2))
    lift = jnp.transpose(face_lift, (2, 0, 1))
    labels = cluster_labels.reshape(1, n.elements)

    field = ((n.basis, n.width), F32)
    grid = ((n.rows, n.cols4), F32)
    pack = ((n.half, LANES), F32)
    peer = ((HALO_PEER, n.rows_pad), F32)
    left_t = ((n.left_rows, 3 * KB), BF16)
    rot_rows = up(3 * n.fm, LANES)
    right_t = pltpu.VMEM((3 * KB, n.width), BF16)
    spread_t = pltpu.VMEM((n.left_rows, n.width), F32)
    held_t = spread_t
    turned_t = pltpu.VMEM((n.slot_cols - LANES, n.rows_pad), F32)
    solved_t = pltpu.VMEM((n.fm, n.width), F32)
    own_stack = pltpu.VMEM((2 * LANES, n.width), BF16)
    rot_stack = pltpu.VMEM((2 * rot_rows, n.width), BF16)
    pad_t = pltpu.VMEM((n.left_rows, LANES), F32)

    slots = [send_element, send_face]
    kept = [project, stiffness, dof, star, lift, face_rotate, local, remote, labels,
            neighbour_index, neighbour_face, neighbour_orient]
    outs = call(
        first_kernel, n, slots + kept,
        [field, field, grid, pack, pack] + [peer] * n.subs + [left_t, ((8, n.slot_cols), jnp.int32)]
        + [(x.shape, x.dtype) for x in kept],
        [right_t, spread_t, held_t, pad_t, turned_t]
        + [pltpu.VMEM(x.shape, x.dtype) for x in slots] + [pltpu.SemaphoreType.DMA((FAR,))],
        far_in=True)
    first, second, table, near, far = outs[:5]
    peers = outs[5 : 5 + n.subs]
    left_one, sends = outs[5 + n.subs : 7 + n.subs]
    project, stiffness, dof, star, lift, face_rotate, local, remote, labels, index, face, orient = outs[7 + n.subs :]
    got = exchange(near, far, peers)
    part, found, left_two, lift_own, lift_rot, masks = call(
        second_kernel, n,
        [first, table, project, stiffness, star, lift, face_rotate, local, index, face, orient],
        [field, grid, left_t, ((2 * n.basis, 2 * LANES), BF16), ((2 * n.basis, 2 * rot_rows), BF16),
         ((3 * n.fm, n.elements), BF16)],
        [right_t, spread_t, pad_t, solved_t, own_stack]
        + [pltpu.VMEM(s, F32) for s in ((rot_rows, LANES), (2 * n.basis, rot_rows), (LANES, LANES), (3 * n.fm, n.elements))])
    outs = call(
        third_kernel, n,
        got + [found, index, remote, masks, lift_rot, part, dof, labels, second, star, left_one, sends],
        [field, field, grid, grid, pack, pack] + [peer] * n.subs,
        [right_t, spread_t, held_t, solved_t, rot_stack, turned_t])
    later, middle, traces, table, near, far = outs[:6]
    got = exchange(near, far, outs[6:])
    part, found = call(
        fourth_kernel, n,
        [first, second, later, middle, labels, star, left_two, local, lift_own, table, index, face, traces],
        [field, grid], [right_t, spread_t, solved_t, own_stack])
    (out,) = call(
        fifth_kernel, n, got + [found, index, remote, masks, lift_rot, part],
        [((n.nvar, n.basis, n.elements), F32)],
        [pltpu.VMEM(*grid), solved_t, rot_stack, turned_t, pltpu.VMEM((n.nvar, n.basis, n.elements), F32),
         pltpu.SemaphoreType.DMA((n.nvar,))], far_out=True)
    return jnp.transpose(out, (1, 0, 2))


def solution(mesh):
    cells = ("dom", "sub")
    in_specs = (
        P(None, None, cells),
        P(),
        P(),
        P(),
        P(),
        P(None, None, None, cells),
        P(None, None, None, cells),
        P(None, None, None, cells),
        P(cells),
        P(None, cells),
        P(None, cells),
        P(None, cells),
        P(cells, None),
        P(cells, None),
    )
    out_specs = P(None, None, cells)
    return jax.shard_map(per_device, mesh=mesh, in_specs=in_specs, out_specs=out_specs, check_vma=False)
```

time: 37.6 us -> 36.1 us (0.960)
  the two profiles are of different devices: /device:TPU:6 before, /device:TPU:4 now
where the time goes in v2:
time: 36.1 us; the launch traced here: 35.9 us
  Pallas kernels  17.1 us (47%)
  starting transfers between devices  15 us (42%)
  waiting for transfers between devices  3.78 us (10%)
    pallas_call x5, Pallas kernels, call(): pl.pallas_call(body, out_shape=[(far if far_out else near)(s, t) for s, t...  17.1 us
    ppermute x10, starting transfers between devices, along(): lax.ppermute(value, axis, [(i, j if 0 <= j < count else i) for i, j in pa...  15 us
    ppermute x10, waiting for transfers between devices, along(): lax.ppermute(value, axis, [(i, j if 0 <= j < count else i) for i, j in pa...  3.78 us
  transfers between devices with their start and end apart: 10, of which 2 were waited for; matrix products, arithmetic and copies ran while one was open for 0% of the time, Pallas kernels for 9%

profile of v2, /device:TPU:4, one launch (start us, length us, event | category | flops | bytes accessed | tf_op | source)
XLA Modules:
  0.0 35.9 jit_solution(10051864553486932973)
XLA Ops:
  0.0 6.1 %shard_map.136 = (f32[56,1152]{1,0:T(8,128)S(1)}, f32[56,1152]{1,0:T(8,128)S(1)}, f32[216,512]{1,0:T(8,128)S(1)}, f32[112,128]{1,0:T(8,128)S(1)}, f32[112,128]{1...) custom-call(s32[1,160]{1,0:T(1,128)} %refs_0_.1, ...), custom_call_target="tpu_custom_call" | custom-call | tf_op jit(solution)/shard_map/pallas_call | solution.py:420
  6.1 0.1 collective-permute-start
  6.2 3.4 %collective-permute-start.1 = (f32[112,128]{1,0:T(8,128)S(1)}, f32[112,128]{1,0:T(8,128)S(1)}, u32[]{:S(2)}, u32[]{:S(2)}) collective-permute-start(f32[112,128]{1,0:T(8,128)S(1)} %get-tuple-element.47), channel_id=1, source_target_pairs={{0,0},{4,8},{8,4},{12,16},{16,12},{20,24},{24,20},{28,28},{1,1},{5... | collective-permute-start | bytes 172040 | tf_op jit(solution)/shard_map/ppermute | solution.py:433
  9.6 1.6 %collective-permute-start.2 = (f32[8,256]{1,0:T(8,128)S(1)}, f32[8,256]{1,0:T(8,128)S(1)}, u32[]{:S(2)}, u32[]{:S(2)}) collective-permute-start(f32[8,256]{1,0:T(8,128)S(1)} %get-tuple-element.49), channel_id=1, source_target_pairs={{0,1},{1,0},{2,3},{3,2},{4,5},{5,4},{6,7},{7,6},{8,9},{9,8},{10,11... | collective-permute-start | bytes 24584 | tf_op jit(solution)/shard_map/ppermute | solution.py:433
  11.2 2.6 %collective-permute-start.3 = (f32[8,256]{1,0:T(8,128)S(1)}, f32[8,256]{1,0:T(8,128)S(1)}, u32[]{:S(2)}, u32[]{:S(2)}) collective-permute-start(f32[8,256]{1,0:T(8,128)S(1)} %get-tuple-element.50), channel_id=1, source_target_pairs={{0,2},{1,3},{2,0},{3,1},{4,6},{5,7},{6,4},{7,5},{8,10},{9,11},{10,... | collective-permute-start | bytes 24584 | tf_op jit(solution)/shard_map/ppermute | solution.py:433
  13.8 0.2 collective-permute-start.4
  14.0 1.8 %shard_map.137 = (f32[56,1152]{1,0:T(8,128)S(1)}, f32[216,512]{1,0:T(8,128)S(1)}, bf16[264,192]{1,0:T(8,128)(2,1)S(1)}, bf16[112,256]{1,0:T(8,128)(2,1)S(1)}, bf...) custom-call(f32[56,1152]{1,0:T(8,128)S(1)} %get-tuple-element.52.refs_0_, ...), custom_call_target="tpu_custom_call" | custom-call | tf_op jit(solution)/shard_map/pallas_call | solution.py:420
  15.8 0.0 collective-permute-done.2.refs_3_
  15.9 0.0 collective-permute-done.3.refs_4_
  15.9 3.4 %collective-permute-done.4.refs_5_ = f32[8,256]{1,0:T(8,128)S(1)} collective-permute-done((f32[8,256]{1,0:T(8,128)S(1)}, f32[8,256]{1,0:T(8,128)S(1)}, u32[]{:S(2)}, u32[]{:S(2)}) %collective-permute-start.4) | collective-permute-done | bytes 8224 | tf_op jit(solution)/shard_map/ppermute | solution.py:433
  19.3 0.0 collective-permute-done.refs_0_
  19.3 0.0 collective-permute-done.1.refs_1_
  19.3 5.8 %shard_map.138 = (f32[56,1152]{1,0:T(8,128)S(1)}, f32[56,1152]{1,0:T(8,128)S(1)}, f32[216,512]{1,0:T(8,128)S(1)}, f32[216,512]{1,0:T(8,128)S(1)}, f32[112,128]{1...) custom-call(f32[112,128]{1,0:T(8,128)S(1)} %collective-permute-done., ...), custom_call_target="tpu_custom_call" | custom-call | tf_op jit(solution)/shard_map/pallas_call | solution.py:420
  25.1 0.1 collective-permute-start.5
  25.2 2.5 %collective-permute-start.6 = (f32[112,128]{1,0:T(8,128)S(1)}, f32[112,128]{1,0:T(8,128)S(1)}, u32[]{:S(2)}, u32[]{:S(2)}) collective-permute-start(f32[112,128]{1,0:T(8,128)S(1)} %get-tuple-element.74), channel_id=1, source_target_pairs={{0,0},{4,8},{8,4},{12,16},{16,12},{20,24},{24,20},{28,28},{1,1},{5... | collective-permute-start | bytes 172040 | tf_op jit(solution)/shard_map/ppermute | solution.py:433
  27.7 0.1 collective-permute-start.7
  27.8 0.8 %collective-permute-start.8 = (f32[8,256]{1,0:T(8,128)S(1)}, f32[8,256]{1,0:T(8,128)S(1)}, u32[]{:S(2)}, u32[]{:S(2)}) collective-permute-start(f32[8,256]{1,0:T(8,128)S(1)} %get-tuple-element.77), channel_id=1, source_target_pairs={{0,2},{1,3},{2,0},{3,1},{4,6},{5,7},{6,4},{7,5},{8,10},{9,11},{10,... | collective-permute-start | bytes 24584 | tf_op jit(solution)/shard_map/ppermute | solution.py:433
  28.6 3.6 %collective-permute-start.9 = (f32[8,256]{1,0:T(8,128)S(1)}, f32[8,256]{1,0:T(8,128)S(1)}, u32[]{:S(2)}, u32[]{:S(2)}) collective-permute-start(f32[8,256]{1,0:T(8,128)S(1)} %get-tuple-element.78), channel_id=1, source_target_pairs={{0,3},{1,2},{2,1},{3,0},{4,7},{5,6},{6,5},{7,4},{8,11},{9,10},{10,... | collective-permute-start | bytes 24584 | tf_op jit(solution)/shard_map/ppermute | solution.py:433
  32.1 1.5 %shard_map.139 = (f32[56,1152]{1,0:T(8,128)S(1)}, f32[216,512]{1,0:T(8,128)S(1)}) custom-call(f32[56,1152]{1,0:T(8,128)S(1)} %get-tuple-element.52.refs_0_, f32[56,1152]{1,0:T(8,128)S(1)} %get-tuple-element.70.refs_14_.refs_1_, f32[56,1152]{1,0:T(8,128)S(1)} %get-tuple-element.79.refs_2_, f32[56,1152]{1,0:T(8,128)S(1)} %get-tuple-element.80.refs_3_, ...), custom_call_target="tpu_custom_call" | custom-call | tf_op jit(solution)/shard_map/pallas_call | solution.py:420
  33.6 0.0 collective-permute-done.7.refs_3_
  33.6 0.0 collective-permute-done.8.refs_4_
  33.6 0.4 %collective-permute-done.9.refs_5_ = f32[8,256]{1,0:T(8,128)S(1)} collective-permute-done((f32[8,256]{1,0:T(8,128)S(1)}, f32[8,256]{1,0:T(8,128)S(1)}, u32[]{:S(2)}, u32[]{:S(2)}) %collective-permute-start.9) | collective-permute-done | bytes 8224 | tf_op jit(solution)/shard_map/ppermute | solution.py:433
  34.0 0.0 collective-permute-done.5.refs_0_
  34.0 0.0 collective-permute-done.6.refs_1_
  34.0 1.9 %shard_map.140 = f32[9,56,128]{2,1,0:T(8,128)} custom-call(f32[112,128]{1,0:T(8,128)S(1)} %collective-permute-done.5.refs_0_, f32[112,128]{1,0:T(8,128)S(1)} %collective-permute-done.6.refs_1_, f32[8,256]{1,0:T(8,128)S(1)} %get-tuple-element.75.refs_2_, f32[8,256]{1,0:T(8,128)S(1)} %collective-permute-done.7.refs_3_, ...), custom_call_target="tpu_custom_call" | custom-call | tf_op jit(solution)/shard_map/pallas_call | solution.py:420
Async XLA Ops:
  6.1 13.2 %collective-permute-start = (f32[112,128]{1,0:T(8,128)S(1)}, f32[112,128]{1,0:T(8,128)S(1)}, u32[]{:S(2)}, u32[]{:S(2)}) collective-permute-start(f32[112,128]{1,0:T(8,128)S(1)} %get-tuple-element.46), channel_id=1, source_target_pairs={{0,4},{4,0},{8,12},{12,8},{16,20},{20,16},{24,28},{28,24},{1,5},{5... | collective-permute-start | bytes 172040 | tf_op jit(solution)/shard_map/ppermute | solution.py:433
  6.2 13.1 %collective-permute-start.1 = (f32[112,128]{1,0:T(8,128)S(1)}, f32[112,128]{1,0:T(8,128)S(1)}, u32[]{:S(2)}, u32[]{:S(2)}) collective-permute-start(f32[112,128]{1,0:T(8,128)S(1)} %get-tuple-element.47), channel_id=1, source_target_pairs={{0,0},{4,8},{8,4},{12,16},{16,12},{20,24},{24,20},{28,28},{1,1},{5... | collective-permute-start | bytes 172040 | tf_op jit(solution)/shard_map/ppermute | solution.py:433
  9.6 6.3 %collective-permute-start.2 = (f32[8,256]{1,0:T(8,128)S(1)}, f32[8,256]{1,0:T(8,128)S(1)}, u32[]{:S(2)}, u32[]{:S(2)}) collective-permute-start(f32[8,256]{1,0:T(8,128)S(1)} %get-tuple-element.49), channel_id=1, source_target_pairs={{0,1},{1,0},{2,3},{3,2},{4,5},{5,4},{6,7},{7,6},{8,9},{9,8},{10,11... | collective-permute-start | bytes 24584 | tf_op jit(solution)/shard_map/ppermute | solution.py:433
  11.2 4.6 %collective-permute-start.3 = (f32[8,256]{1,0:T(8,128)S(1)}, f32[8,256]{1,0:T(8,128)S(1)}, u32[]{:S(2)}, u32[]{:S(2)}) collective-permute-start(f32[8,256]{1,0:T(8,128)S(1)} %get-tuple-element.50), channel_id=1, source_target_pairs={{0,2},{1,3},{2,0},{3,1},{4,6},{5,7},{6,4},{7,5},{8,10},{9,11},{10,... | collective-permute-start | bytes 24584 | tf_op jit(solution)/shard_map/ppermute | solution.py:433
  13.8 5.4 %collective-permute-start.4 = (f32[8,256]{1,0:T(8,128)S(1)}, f32[8,256]{1,0:T(8,128)S(1)}, u32[]{:S(2)}, u32[]{:S(2)}) collective-permute-start(f32[8,256]{1,0:T(8,128)S(1)} %get-tuple-element.51), channel_id=1, source_target_pairs={{0,3},{1,2},{2,1},{3,0},{4,7},{5,6},{6,5},{7,4},{8,11},{9,10},{10,... | collective-permute-start | bytes 24584 | tf_op jit(solution)/shard_map/ppermute | solution.py:433
  25.1 8.9 %collective-permute-start.5 = (f32[112,128]{1,0:T(8,128)S(1)}, f32[112,128]{1,0:T(8,128)S(1)}, u32[]{:S(2)}, u32[]{:S(2)}) collective-permute-start(f32[112,128]{1,0:T(8,128)S(1)} %get-tuple-element.73), channel_id=1, source_target_pairs={{0,4},{4,0},{8,12},{12,8},{16,20},{20,16},{24,28},{28,24},{1,5},{5... | collective-permute-start | bytes 172040 | tf_op jit(solution)/shard_map/ppermute | solution.py:433
  25.2 8.9 %collective-permute-start.6 = (f32[112,128]{1,0:T(8,128)S(1)}, f32[112,128]{1,0:T(8,128)S(1)}, u32[]{:S(2)}, u32[]{:S(2)}) collective-permute-start(f32[112,128]{1,0:T(8,128)S(1)} %get-tuple-element.74), channel_id=1, source_target_pairs={{0,0},{4,8},{8,4},{12,16},{16,12},{20,24},{24,20},{28,28},{1,1},{5... | collective-permute-start | bytes 172040 | tf_op jit(solution)/shard_map/ppermute | solution.py:433
  27.7 5.9 %collective-permute-start.7 = (f32[8,256]{1,0:T(8,128)S(1)}, f32[8,256]{1,0:T(8,128)S(1)}, u32[]{:S(2)}, u32[]{:S(2)}) collective-permute-start(f32[8,256]{1,0:T(8,128)S(1)} %get-tuple-element.76), channel_id=1, source_target_pairs={{0,1},{1,0},{2,3},{3,2},{4,5},{5,4},{6,7},{7,6},{8,9},{9,8},{10,11... | collective-permute-start | bytes 24584 | tf_op jit(solution)/shard_map/ppermute | solution.py:433
  27.8 5.9 %collective-permute-start.8 = (f32[8,256]{1,0:T(8,128)S(1)}, f32[8,256]{1,0:T(8,128)S(1)}, u32[]{:S(2)}, u32[]{:S(2)}) collective-permute-start(f32[8,256]{1,0:T(8,128)S(1)} %get-tuple-element.77), channel_id=1, source_target_pairs={{0,2},{1,3},{2,0},{3,1},{4,6},{5,7},{6,4},{7,5},{8,10},{9,11},{10,... | collective-permute-start | bytes 24584 | tf_op jit(solution)/shard_map/ppermute | solution.py:433
  28.6 5.4 %collective-permute-start.9 = (f32[8,256]{1,0:T(8,128)S(1)}, f32[8,256]{1,0:T(8,128)S(1)}, u32[]{:S(2)}, u32[]{:S(2)}) collective-permute-start(f32[8,256]{1,0:T(8,128)S(1)} %get-tuple-element.78), channel_id=1, source_target_pairs={{0,3},{1,2},{2,1},{3,0},{4,7},{5,6},{6,5},{7,4},{8,11},{9,10},{10,... | collective-permute-start | bytes 24584 | tf_op jit(solution)/shard_map/ppermute | solution.py:433

commit v3 on v2

--- a/solution.py
+++ b/solution.py
@@ -286,12 +286,15 @@
     for o in range(3):
         square[...] = jnp.zeros_like(square)
         square[: n.fbasis, : n.fbasis] = face_rotate[o]
-        turn = square[...].T[: n.mp, :]
-        turn = turn[:, : n.mp]
+        tall[o * n.mp : (o + 1) * n.mp, :LANES] = square[...].T[: n.mp, :]
+    turn_hi, turn_lo = halves(tall[: 3 * n.mp, : n.mp])
+    side = jnp.concatenate([base[g * n.mp : (g + 1) * n.mp, :] for g in range(4)], axis=1)
+    side_hi, side_lo = halves(side)
+    both = dot(turn_hi, side_hi) + (dot(turn_lo, side_hi) + dot(turn_hi, side_lo))
+    for o in range(3):
         for g in range(4):
             r = o * n.fm + g * n.mp
-            wide[r : r + n.mp, :] = jnp.dot(turn, base[g * n.mp : (g + 1) * n.mp, :],
-                                            precision=lax.Precision.HIGHEST, preferred_element_type=F32)
+            wide[r : r + n.mp, :] = both[o * n.mp : (o + 1) * n.mp, g * LANES : (g + 1) * LANES]
     blocks = wide.shape[0] // LANES
     turned = jnp.concatenate([wide[i * LANES : (i + 1) * LANES, :].T[: n.basis, :] for i in range(blocks)], axis=1)
     lift_rows(n, lift_turned, tall, turned)

time: 36.1 us -> 36.1 us (level)
  the two profiles are of different devices: /device:TPU:4 before, /device:TPU:30 now
where the time goes in v3:
time: 36.1 us; the launch traced here: 35.9 us
  Pallas kernels  17 us (47%)
  starting transfers between devices  15 us (42%)
  waiting for transfers between devices  3.84 us (11%)
    pallas_call x5, Pallas kernels, call(): pl.pallas_call(body, out_shape=[(far if far_out else near)(s, t) for s, t...  17 us
    ppermute x10, starting transfers between devices, along(): lax.ppermute(value, axis, [(i, j if 0 <= j < count else i) for i, j in pa...  15 us
    ppermute x10, waiting for transfers between devices, along(): lax.ppermute(value, axis, [(i, j if 0 <= j < count else i) for i, j in pa...  3.84 us
  transfers between devices with their start and end apart: 10, of which 2 were waited for; matrix products, arithmetic and copies ran while one was open for 0% of the time, Pallas kernels for 9%

profile of v3, /device:TPU:30, one launch (start us, length us, event | category | flops | bytes accessed | tf_op | source)
XLA Modules:
  0.0 35.9 jit_solution(12556477231802547581)
XLA Ops:
  0.0 6.1 %shard_map.136 = (f32[56,1152]{1,0:T(8,128)S(1)}, f32[56,1152]{1,0:T(8,128)S(1)}, f32[216,512]{1,0:T(8,128)S(1)}, f32[112,128]{1,0:T(8,128)S(1)}, f32[112,128]{1...) custom-call(s32[1,160]{1,0:T(1,128)} %refs_0_.1, ...), custom_call_target="tpu_custom_call" | custom-call | tf_op jit(solution)/shard_map/pallas_call | solution.py:423
  6.1 0.1 collective-permute-start
  6.2 2.5 %collective-permute-start.1 = (f32[112,128]{1,0:T(8,128)S(1)}, f32[112,128]{1,0:T(8,128)S(1)}, u32[]{:S(2)}, u32[]{:S(2)}) collective-permute-start(f32[112,128]{1,0:T(8,128)S(1)} %get-tuple-element.47), channel_id=1, source_target_pairs={{0,0},{4,8},{8,4},{12,16},{16,12},{20,24},{24,20},{28,28},{1,1},{5... | collective-permute-start | bytes 172040 | tf_op jit(solution)/shard_map/ppermute | solution.py:436
  8.7 0.5 %collective-permute-start.2 = (f32[8,256]{1,0:T(8,128)S(1)}, f32[8,256]{1,0:T(8,128)S(1)}, u32[]{:S(2)}, u32[]{:S(2)}) collective-permute-start(f32[8,256]{1,0:T(8,128)S(1)} %get-tuple-element.49), channel_id=1, source_target_pairs={{0,1},{1,0},{2,3},{3,2},{4,5},{5,4},{6,7},{7,6},{8,9},{9,8},{10,11... | collective-permute-start | bytes 24584 | tf_op jit(solution)/shard_map/ppermute | solution.py:436
  9.2 0.3 collective-permute-start.3
  9.5 3.6 %collective-permute-start.4 = (f32[8,256]{1,0:T(8,128)S(1)}, f32[8,256]{1,0:T(8,128)S(1)}, u32[]{:S(2)}, u32[]{:S(2)}) collective-permute-start(f32[8,256]{1,0:T(8,128)S(1)} %get-tuple-element.51), channel_id=1, source_target_pairs={{0,3},{1,2},{2,1},{3,0},{4,7},{5,6},{6,5},{7,4},{8,11},{9,10},{10,... | collective-permute-start | bytes 24584 | tf_op jit(solution)/shard_map/ppermute | solution.py:436
  13.1 1.7 %shard_map.137 = (f32[56,1152]{1,0:T(8,128)S(1)}, f32[216,512]{1,0:T(8,128)S(1)}, bf16[264,192]{1,0:T(8,128)(2,1)S(1)}, bf16[112,256]{1,0:T(8,128)(2,1)S(1)}, bf...) custom-call(f32[56,1152]{1,0:T(8,128)S(1)} %get-tuple-element.52.refs_0_, ...), custom_call_target="tpu_custom_call" | custom-call | tf_op jit(solution)/shard_map/pallas_call | solution.py:423
  14.9 0.0 collective-permute-done.2.refs_3_
  14.9 0.0 collective-permute-done.3.refs_4_
  14.9 0.1 collective-permute-done.4.refs_5_
  15.0 0.0 collective-permute-done.refs_0_
  15.0 0.0 collective-permute-done.1.refs_1_
  15.0 5.8 %shard_map.138 = (f32[56,1152]{1,0:T(8,128)S(1)}, f32[56,1152]{1,0:T(8,128)S(1)}, f32[216,512]{1,0:T(8,128)S(1)}, f32[216,512]{1,0:T(8,128)S(1)}, f32[112,128]{1...) custom-call(f32[112,128]{1,0:T(8,128)S(1)} %collective-permute-done., ...), custom_call_target="tpu_custom_call" | custom-call | tf_op jit(solution)/shard_map/pallas_call | solution.py:423
  20.8 0.1 collective-permute-start.5
  20.9 3.4 %collective-permute-start.6 = (f32[112,128]{1,0:T(8,128)S(1)}, f32[112,128]{1,0:T(8,128)S(1)}, u32[]{:S(2)}, u32[]{:S(2)}) collective-permute-start(f32[112,128]{1,0:T(8,128)S(1)} %get-tuple-element.74), channel_id=1, source_target_pairs={{0,0},{4,8},{8,4},{12,16},{16,12},{20,24},{24,20},{28,28},{1,1},{5... | collective-permute-start | bytes 172040 | tf_op jit(solution)/shard_map/ppermute | solution.py:436
  24.3 0.4 %collective-permute-start.7 = (f32[8,256]{1,0:T(8,128)S(1)}, f32[8,256]{1,0:T(8,128)S(1)}, u32[]{:S(2)}, u32[]{:S(2)}) collective-permute-start(f32[8,256]{1,0:T(8,128)S(1)} %get-tuple-element.76), channel_id=1, source_target_pairs={{0,1},{1,0},{2,3},{3,2},{4,5},{5,4},{6,7},{7,6},{8,9},{9,8},{10,11... | collective-permute-start | bytes 24584 | tf_op jit(solution)/shard_map/ppermute | solution.py:436
  24.7 3.8 %collective-permute-start.8 = (f32[8,256]{1,0:T(8,128)S(1)}, f32[8,256]{1,0:T(8,128)S(1)}, u32[]{:S(2)}, u32[]{:S(2)}) collective-permute-start(f32[8,256]{1,0:T(8,128)S(1)} %get-tuple-element.77), channel_id=1, source_target_pairs={{0,2},{1,3},{2,0},{3,1},{4,6},{5,7},{6,4},{7,5},{8,10},{9,11},{10,... | collective-permute-start | bytes 24584 | tf_op jit(solution)/shard_map/ppermute | solution.py:436
  28.5 0.2 collective-permute-start.9
  28.8 1.5 %shard_map.139 = (f32[56,1152]{1,0:T(8,128)S(1)}, f32[216,512]{1,0:T(8,128)S(1)}) custom-call(f32[56,1152]{1,0:T(8,128)S(1)} %get-tuple-element.52.refs_0_, f32[56,1152]{1,0:T(8,128)S(1)} %get-tuple-element.70.refs_14_.refs_1_, f32[56,1152]{1,0:T(8,128)S(1)} %get-tuple-element.79.refs_2_, f32[56,1152]{1,0:T(8,128)S(1)} %get-tuple-element.80.refs_3_, ...), custom_call_target="tpu_custom_call" | custom-call | tf_op jit(solution)/shard_map/pallas_call | solution.py:423
  30.3 0.0 collective-permute-done.7.refs_3_
  30.3 0.0 collective-permute-done.8.refs_4_
  30.3 3.7 %collective-permute-done.9.refs_5_ = f32[8,256]{1,0:T(8,128)S(1)} collective-permute-done((f32[8,256]{1,0:T(8,128)S(1)}, f32[8,256]{1,0:T(8,128)S(1)}, u32[]{:S(2)}, u32[]{:S(2)}) %collective-permute-start.9) | collective-permute-done | bytes 8224 | tf_op jit(solution)/shard_map/ppermute | solution.py:436
  34.0 0.0 collective-permute-done.5.refs_0_
  34.0 0.0 collective-permute-done.6.refs_1_
  34.0 1.9 %shard_map.140 = f32[9,56,128]{2,1,0:T(8,128)} custom-call(f32[112,128]{1,0:T(8,128)S(1)} %collective-permute-done.5.refs_0_, f32[112,128]{1,0:T(8,128)S(1)} %collective-permute-done.6.refs_1_, f32[8,256]{1,0:T(8,128)S(1)} %get-tuple-element.75.refs_2_, f32[8,256]{1,0:T(8,128)S(1)} %collective-permute-done.7.refs_3_, ...), custom_call_target="tpu_custom_call" | custom-call | tf_op jit(solution)/shard_map/pallas_call | solution.py:423
Async XLA Ops:
  6.1 8.9 %collective-permute-start = (f32[112,128]{1,0:T(8,128)S(1)}, f32[112,128]{1,0:T(8,128)S(1)}, u32[]{:S(2)}, u32[]{:S(2)}) collective-permute-start(f32[112,128]{1,0:T(8,128)S(1)} %get-tuple-element.46), channel_id=1, source_target_pairs={{0,4},{4,0},{8,12},{12,8},{16,20},{20,16},{24,28},{28,24},{1,5},{5... | collective-permute-start | bytes 172040 | tf_op jit(solution)/shard_map/ppermute | solution.py:436
  6.2 8.8 %collective-permute-start.1 = (f32[112,128]{1,0:T(8,128)S(1)}, f32[112,128]{1,0:T(8,128)S(1)}, u32[]{:S(2)}, u32[]{:S(2)}) collective-permute-start(f32[112,128]{1,0:T(8,128)S(1)} %get-tuple-element.47), channel_id=1, source_target_pairs={{0,0},{4,8},{8,4},{12,16},{16,12},{20,24},{24,20},{28,28},{1,1},{5... | collective-permute-start | bytes 172040 | tf_op jit(solution)/shard_map/ppermute | solution.py:436
  8.7 6.2 %collective-permute-start.2 = (f32[8,256]{1,0:T(8,128)S(1)}, f32[8,256]{1,0:T(8,128)S(1)}, u32[]{:S(2)}, u32[]{:S(2)}) collective-permute-start(f32[8,256]{1,0:T(8,128)S(1)} %get-tuple-element.49), channel_id=1, source_target_pairs={{0,1},{1,0},{2,3},{3,2},{4,5},{5,4},{6,7},{7,6},{8,9},{9,8},{10,11... | collective-permute-start | bytes 24584 | tf_op jit(solution)/shard_map/ppermute | solution.py:436
  9.2 5.7 %collective-permute-start.3 = (f32[8,256]{1,0:T(8,128)S(1)}, f32[8,256]{1,0:T(8,128)S(1)}, u32[]{:S(2)}, u32[]{:S(2)}) collective-permute-start(f32[8,256]{1,0:T(8,128)S(1)} %get-tuple-element.50), channel_id=1, source_target_pairs={{0,2},{1,3},{2,0},{3,1},{4,6},{5,7},{6,4},{7,5},{8,10},{9,11},{10,... | collective-permute-start | bytes 24584 | tf_op jit(solution)/shard_map/ppermute | solution.py:436
  9.5 5.4 %collective-permute-start.4 = (f32[8,256]{1,0:T(8,128)S(1)}, f32[8,256]{1,0:T(8,128)S(1)}, u32[]{:S(2)}, u32[]{:S(2)}) collective-permute-start(f32[8,256]{1,0:T(8,128)S(1)} %get-tuple-element.51), channel_id=1, source_target_pairs={{0,3},{1,2},{2,1},{3,0},{4,7},{5,6},{6,5},{7,4},{8,11},{9,10},{10,... | collective-permute-start | bytes 24584 | tf_op jit(solution)/shard_map/ppermute | solution.py:436
  20.8 13.2 %collective-permute-start.5 = (f32[112,128]{1,0:T(8,128)S(1)}, f32[112,128]{1,0:T(8,128)S(1)}, u32[]{:S(2)}, u32[]{:S(2)}) collective-permute-start(f32[112,128]{1,0:T(8,128)S(1)} %get-tuple-element.73), channel_id=1, source_target_pairs={{0,4},{4,0},{8,12},{12,8},{16,20},{20,16},{24,28},{28,24},{1,5},{5... | collective-permute-start | bytes 172040 | tf_op jit(solution)/shard_map/ppermute | solution.py:436
  20.9 13.1 %collective-permute-start.6 = (f32[112,128]{1,0:T(8,128)S(1)}, f32[112,128]{1,0:T(8,128)S(1)}, u32[]{:S(2)}, u32[]{:S(2)}) collective-permute-start(f32[112,128]{1,0:T(8,128)S(1)} %get-tuple-element.74), channel_id=1, source_target_pairs={{0,0},{4,8},{8,4},{12,16},{16,12},{20,24},{24,20},{28,28},{1,1},{5... | collective-permute-start | bytes 172040 | tf_op jit(solution)/shard_map/ppermute | solution.py:436
  24.3 5.9 %collective-permute-start.7 = (f32[8,256]{1,0:T(8,128)S(1)}, f32[8,256]{1,0:T(8,128)S(1)}, u32[]{:S(2)}, u32[]{:S(2)}) collective-permute-start(f32[8,256]{1,0:T(8,128)S(1)} %get-tuple-element.76), channel_id=1, source_target_pairs={{0,1},{1,0},{2,3},{3,2},{4,5},{5,4},{6,7},{7,6},{8,9},{9,8},{10,11... | collective-permute-start | bytes 24584 | tf_op jit(solution)/shard_map/ppermute | solution.py:436
  24.7 5.5 %collective-permute-start.8 = (f32[8,256]{1,0:T(8,128)S(1)}, f32[8,256]{1,0:T(8,128)S(1)}, u32[]{:S(2)}, u32[]{:S(2)}) collective-permute-start(f32[8,256]{1,0:T(8,128)S(1)} %get-tuple-element.77), channel_id=1, source_target_pairs={{0,2},{1,3},{2,0},{3,1},{4,6},{5,7},{6,4},{7,5},{8,10},{9,11},{10,... | collective-permute-start | bytes 24584 | tf_op jit(solution)/shard_map/ppermute | solution.py:436
  28.5 5.4 %collective-permute-start.9 = (f32[8,256]{1,0:T(8,128)S(1)}, f32[8,256]{1,0:T(8,128)S(1)}, u32[]{:S(2)}, u32[]{:S(2)}) collective-permute-start(f32[8,256]{1,0:T(8,128)S(1)} %get-tuple-element.78), channel_id=1, source_target_pairs={{0,3},{1,2},{2,1},{3,0},{4,7},{5,6},{6,5},{7,4},{8,11},{9,10},{10,... | collective-permute-start | bytes 24584 | tf_op jit(solution)/shard_map/ppermute | solution.py:436
